TPU v7x, 32 devices: a whole 2x2x4 slice. The times are simulated.
32 devices in a mesh: dp: 4 (over y, x), ctx: 2 (over core), tensor: 4 (over z).
Axes of the slice: x: 2, y: 2, z: 4, core: 2. Of those that a mesh axis runs over, the one named last changes fastest.
Arguments:
- hidden: bfloat16 [16, 512, 768], P('dp', 'ctx'), may hold values from -6 to 6
- query: bfloat16 [16, 512, 768], P('dp', 'ctx'), may hold values from -6 to 6
- memory: bfloat16 [16, 384, 768], P('dp', 'ctx'), may hold values from -6 to 6
- cot_hidden: bfloat16 [16, 512, 768], P('dp', 'ctx'), may hold values from -6 to 6
- cot_query: bfloat16 [16, 512, 768], P('dp', 'ctx'), may hold values from -6 to 6
- lengths: int32 [16], P('dp'), may hold values from 64 to 512, as said below
- ranks: int32 [16, 512], P('dp'), may hold values from 0 to 511, each once within a row
- segments: int32 [16, 896], P('dp'), may hold values from 0 to 3, never falling along the last dimension, each value on 1 to 448 neighbouring positions
- w_query: bfloat16 [768, 768], P(None, 'tensor'), may hold values from -0.21875 to 0.21875
- w_key: bfloat16 [768, 768], P(None, 'tensor'), may hold values from -0.21875 to 0.21875
- w_value: bfloat16 [768, 768], P(None, 'tensor'), may hold values from -0.21875 to 0.21875
- w_rel: bfloat16 [768, 768], P(None, 'tensor'), may hold values from -0.21875 to 0.21875
- w_out: bfloat16 [768, 768], P('tensor'), may hold values from -4 to 4
- bias_word: float32 [12, 64], P('tensor'), may hold values from -3 to 3
- bias_rel: float32 [12, 64], P('tensor'), may hold values from -3 to 3
- bias_seg: float32 [12, 64], P('tensor'), may hold values from -3 to 3
- seg_embed: float32 [2, 12, 64], P(None, 'tensor'), may hold values from -0.75 to 0.75
- norm1_gain: float32 [768], replicated, may hold values from 0.5 to 1.5
- norm1_bias: float32 [768], replicated, may hold values from -1 to 1
- w_inner: bfloat16 [768, 3072], P(None, 'tensor'), may hold values from -0.21875 to 0.21875
- b_inner: float32 [3072], P('tensor'), may hold values from -1 to 1
- w_outer: bfloat16 [3072, 768], P('tensor'), may hold values from -0.109375 to 0.109375
- b_outer: float32 [768], replicated, may hold values from -1 to 1
- norm2_gain: float32 [768], replicated, may hold values from 0.5 to 1.5
- norm2_bias: float32 [768], replicated, may hold values from -1 to 1
Outputs:
- out_hidden: float32 [16, 512, 768], P('dp', ('ctx', 'tensor'))
- out_query: float32 [16, 512, 768], P('dp', ('ctx', 'tensor'))
- grad_hidden: float32 [16, 512, 768], P('dp', ('ctx', 'tensor'))
- grad_query: float32 [16, 512, 768], P('dp', ('ctx', 'tensor'))
- grad_w_query: float32 [768, 768], P(None, 'tensor')
- grad_w_key: float32 [768, 768], P(None, 'tensor')
- grad_w_value: float32 [768, 768], P(None, 'tensor')
- grad_w_rel: float32 [768, 768], P(None, 'tensor')
- grad_w_out: float32 [768, 768], P('tensor')
- grad_bias_word: float32 [12, 64], P('tensor')
- grad_bias_rel: float32 [12, 64], P('tensor')
- grad_bias_seg: float32 [12, 64], P('tensor')
- grad_seg_embed: float32 [2, 12, 64], P(None, 'tensor')
- grad_norm1_gain: float32 [768], P('tensor')
- grad_norm1_bias: float32 [768], P('tensor')
- grad_w_inner: float32 [768, 3072], P(None, 'tensor')
- grad_b_inner: float32 [3072], P('tensor')
- grad_w_outer: float32 [3072, 768], P('tensor')
- grad_b_outer: float32 [768], P('tensor')
- grad_norm2_gain: float32 [768], P('tensor')
- grad_norm2_bias: float32 [768], P('tensor')
Inputs may be any that keep to these rules, and one draw needn't show every extreme that they name: `lengths`: in each aligned block of 4 sequences one has exactly 512 rows. `ranks`: each row is a permutation of the positions. `segments`: segment ids never fall along a row.
All inputs are finite; a program needn't handle non-finite values.
Results may differ from a plain program's by a relative error of at most 0.025.
Values may be sent and summed in bfloat16 or wider, within the bound.
No kernel may reach another device: no remote copies, remote signals or barrier semaphores. Data moves between devices by JAX's collectives and lax.ppermute only.
A program may use at most 256 MiB of HBM per device.

v0:
```python
from functools import partial
import math

import jax
import jax.numpy as jnp
from jax import lax
from jax.experimental import pallas as pl
from jax.experimental.pallas import tpu as pltpu
from jax.sharding import PartitionSpec as P

D = 768
DH = 64
L = 512
M = 384
KT = M + L
RQ = 256
WIN = RQ + KT
HB = 128
WB = KT + HB
LANES = 128
NEG = -1e30
EPS = 1e-12
bf16 = jnp.bfloat16
f32 = jnp.float32


def dot(a, b):
    return lax.dot_general(a, b, (((1,), (0,)), ((), ())), preferred_element_type=f32)


def dot_nt(a, b):
    return lax.dot_general(a, b, (((1,), (1,)), ((), ())), preferred_element_type=f32)


def dot_tn(a, b):
    return lax.dot_general(a, b, (((0,), (0,)), ((), ())), preferred_element_type=f32)


def iota(shape, dim):
    return lax.broadcasted_iota(jnp.int32, shape, dim)


def row_to_col(row, n):
    return jnp.transpose(jnp.broadcast_to(row, (LANES, n)))


def pad_rows(dst, src, count):
    dst[:count, :] = src
    dst[count:, :] = jnp.zeros((dst.shape[0] - count, dst.shape[1]), dst.dtype)


def seg_parts(qs, se_ref, seg_col, scale):
    d_i = iota((2 * LANES, LANES), 0)
    l_i = iota((2 * LANES, LANES), 1)
    head_of_lane = jnp.where(l_i < 8, 0, jnp.where(l_i < 16, 1, jnp.where((l_i >= 64) & (l_i < 72), 2, -1)))
    pick = ((d_i // DH) == head_of_lane).astype(bf16)
    sides = []
    for s in range(2):
        prod = qs * se_ref[s : s + 1, :] * scale
        hi = prod.astype(bf16)
        lo = (prod - hi.astype(f32)).astype(bf16)
        sides.append(dot(hi, pick) + dot(lo, pick))
    lane = iota(sides[0].shape, 1)
    val = jnp.where((lane & 3) == seg_col, sides[0], sides[1])
    hi = val.astype(bf16).astype(f32)
    lo = val - hi
    return jnp.where((lane & 7) < 4, hi, lo)


def head_mask(h, shape):
    return (iota(shape, 1) // DH) == (h & 1)


def ext_mask(h, shape):
    return (iota(shape, 1) // 8) == (h if h < 2 else 8)


def attn_fwd_kernel(
    meta, hid, qry, mem, hid_o, mem_o, ranks, segs, wq, wk, wv, rk, bw, br, bs, se,
    *rest,
):
    n_t = len(rest) - 12
    att_out = rest[:n_t]
    p_out, kx_out, v_out, wq_s, wk_s, wv_s, key_s, ma_s, word_s, rel_s, ext_s, o_s = rest[n_t:]
    t_me = meta[meta.shape[0] - 2]
    step = pl.program_id(0)
    s = step + meta[meta.shape[0] - 1]
    c = meta[0]
    length = meta[1 + s]

    @pl.when(step == 0)
    def _():
        pad_rows(wq_s, wq[...], 3 * DH)
        pad_rows(wk_s, wk[...], 3 * DH)
        pad_rows(wv_s, wv[...], 3 * DH)

    rm = mem.shape[1]
    rh = hid.shape[1]
    key_s[pl.ds(pl.multiple_of(c * rm, 64), rm), :] = mem[0]
    key_s[pl.ds(pl.multiple_of((1 - c) * rm, 64), rm), :] = mem_o[0]
    key_s[pl.ds(pl.multiple_of(M + c * rh, 64), rh), :] = hid[0]
    key_s[pl.ds(pl.multiple_of(M + (1 - c) * rh, 64), rh), :] = hid_o[0]

    seg_row = segs[pl.ds(s, 1), :]
    own_seg = jnp.where(c == 0, seg_row[:, M : M + RQ], seg_row[:, M + RQ :])
    seg_col = row_to_col(own_seg.astype(f32), RQ).astype(jnp.int32)
    rank_row = ranks[pl.ds(s, 1), :]
    own_rank = jnp.where(c == 0, rank_row[:, :RQ], rank_row[:, RQ:])
    thr_col = row_to_col(own_rank.astype(f32), RQ)[:, :1]
    valid = iota((1, L), 1) < length
    key_rank = jnp.where(valid, rank_row, 1 << 20).astype(f32)
    ma_s[0] = jnp.where(key_rank <= thr_col, 0.0, NEG)
    ma_s[1] = jnp.where(key_rank < thr_col, 0.0, NEG)

    hot = ((iota((LANES, KT), 0) & 3) == seg_row).astype(f32)
    hot = jnp.transpose(hot)
    keys = dot_nt(key_s[...], wk_s[...])
    kx_out[0, :, :LANES] = keys[:, :LANES].astype(bf16)
    kx_out[0, :, LANES : 2 * LANES] = hot.astype(bf16)
    k2 = jnp.where(iota((KT, LANES), 1) < DH, keys[:, LANES:], hot)
    kx_out[0, :, 2 * LANES :] = k2.astype(bf16)
    v_out[0] = dot_nt(key_s[...], wv_s[...]).astype(bf16)

    scale = 1.0 / math.sqrt(DH)
    for a, x_ref in enumerate((hid, qry)):
        q_raw = dot_nt(x_ref[0], wq_s[...])
        word_s[a] = ((q_raw + bw[...]) * scale).astype(bf16)
        rel_s[a] = ((q_raw + br[...]) * scale).astype(bf16)
        ext_s[a] = seg_parts(q_raw + bs[...], se, seg_col, scale).astype(bf16)

    zero_b = jnp.zeros((), bf16)
    hc = 3 * DH

    def stream(a, carry):
        outs = []
        for h in range(3):
            lo = (h // 2) * LANES
            w_h = word_s[a, :, lo : lo + LANES]
            e_h = jnp.where(ext_mask(h, (RQ, LANES)), ext_s[a], zero_b)
            if h < 2:
                qx = jnp.concatenate([jnp.where(head_mask(h, w_h.shape), w_h, zero_b), e_h], 1)
                kx = kx_out[0, :, : 2 * LANES]
            else:
                qx = jnp.where(head_mask(h, w_h.shape), w_h, e_h)
                kx = kx_out[0, :, 2 * LANES :]
            r_h = rel_s[a, :, lo : lo + LANES]
            qr = jnp.where(head_mask(h, r_h.shape), r_h, zero_b)
            content = dot_nt(qx, kx)
            for i0 in (0, HB):
                w0 = HB - i0
                pos = dot_nt(qr[i0 : i0 + HB], rk[w0 : w0 + WB, lo : lo + LANES])
                pos = pltpu.roll(pos, WB - HB, 1, stride=1, stride_axis=0)[:, :KT]
                sc = content[i0 : i0 + HB] + pos
                sc = jnp.concatenate([sc[:, :M], sc[:, M:] + ma_s[a, i0 : i0 + HB, :]], 1)
                top = jnp.max(sc, -1, keepdims=True)
                e = jnp.exp(sc - top)
                inv = 1.0 / jnp.sum(e, -1, keepdims=True)
                p_out[0, h, a, i0 : i0 + HB, :] = (e * inv).astype(bf16)
            outs.append(dot(p_out[0, h, a], v_out[0, :, lo : lo + LANES]))
        o_s[a, :, :LANES] = jnp.where(head_mask(0, outs[0].shape), outs[0], outs[1]).astype(bf16)
        o_s[a, :, LANES:] = outs[2].astype(bf16)
        return carry

    lax.fori_loop(0, 2, stream, 0)
    share_rows(att_out, lambda a, rows: o_s[a, rows, :hc], t_me)


def share_rows(dst, read, t_me):
    rr = RQ // len(dst)
    for k, ref in enumerate(dst):
        rows = pl.ds(pl.multiple_of((t_me ^ k) * rr, rr), rr)
        ref[...] = jnp.concatenate([read(0, rows), read(1, rows)], 1)


def whole(shape):
    zeros = (0,) * len(shape)
    return pl.BlockSpec(shape, lambda s, *_: zeros)


def per_seq(shape, axis=0):
    return pl.BlockSpec(shape, lambda s, *_: tuple(s if d == axis else 0 for d in range(len(shape))))


def from_seq(shape):
    return pl.BlockSpec(shape, lambda s, meta: (s + meta[meta.shape[0] - 1],) + (0,) * (len(shape) - 1))


def by_lane(shape):
    return pl.BlockSpec(shape, lambda s, *_: (0, s))


def attn_fwd(meta, hid, qry, mem, hid_o, mem_o, ranks, segs, wq, wk, wv, rk, bw, br, bs, se, n_t, count):
    _, rh, _ = hid.shape
    rm = mem.shape[1]
    hc = wq.shape[0]
    rr = rh // n_t
    seq = from_seq
    sds = jax.ShapeDtypeStruct
    grid_spec = pltpu.PrefetchScalarGridSpec(
        num_scalar_prefetch=1,
        grid=(count,),
        in_specs=[
            seq((1, rh, D)), seq((1, rh, D)), seq((1, rm, D)), seq((1, rh, D)), seq((1, rm, D)),
            whole(ranks.shape), whole(segs.shape), whole(wq.shape), whole(wk.shape), whole(wv.shape),
            whole(rk.shape), whole(bw.shape), whole(br.shape), whole(bs.shape), whole(se.shape),
        ],
        out_specs=[by_lane((rr, 2 * hc))] * n_t + [
            per_seq((1, 3, 2, rh, KT)), per_seq((1, KT, 3 * LANES)), per_seq((1, KT, 2 * LANES)),
        ],
        scratch_shapes=[
            pltpu.VMEM((2 * LANES, D), bf16), pltpu.VMEM((2 * LANES, D), bf16), pltpu.VMEM((2 * LANES, D), bf16),
            pltpu.VMEM((KT, D), bf16), pltpu.VMEM((2, RQ, L), f32), pltpu.VMEM((2, RQ, 2 * LANES), bf16),
            pltpu.VMEM((2, RQ, 2 * LANES), bf16), pltpu.VMEM((2, RQ, LANES), bf16), pltpu.VMEM((2, RQ, 2 * LANES), bf16),
        ],
    )
    out = pl.pallas_call(
        attn_fwd_kernel,
        grid_spec=grid_spec,
        out_shape=[sds((rr, count * 2 * hc), bf16)] * n_t + [
            sds((count, 3, 2, rh, KT), bf16), sds((count, KT, 3 * LANES), bf16), sds((count, KT, 2 * LANES), bf16),
        ],
        compiler_params=pltpu.CompilerParams(vmem_limit_bytes=56 << 20),
        cost_estimate=pl.CostEstimate(flops=count * 10**10, bytes_accessed=count * 16 * 10**6, transcendentals=count * 10**6),
        name="attn_fwd",
    )(meta, hid, qry, mem, hid_o, mem_o, ranks, segs, wq, wk, wv, rk, bw, br, bs, se)
    return out[:n_t], out[n_t:]


SUM_ROWS = 16


def attn_bwd_kernel(meta, p_in, kx, v, hid, qry, mem, hid_o, mem_o, segs, wq, rk, table, bw, br, bs, se, *rest):
    n_t = (len(rest) - 20) // 2
    datt, dq_out = rest[:n_t], rest[n_t : 2 * n_t]
    (dkv_own, dkv_oth, gw_own, gw_oth, wq_s, key_s, do_s, x_s, word_s, rel_s, qs_s, ds_s, sk_s, dkv_s, dw_s, dr_s, dg_s,
     g_a, gr_a, sm_a) = rest[2 * n_t :]
    t_me = meta[meta.shape[0] - 2]
    step = pl.program_id(0)
    s = step + meta[meta.shape[0] - 1]
    c = meta[0]
    rm = mem.shape[1]
    rh = hid.shape[1]
    hc = 3 * DH

    @pl.when(step == 0)
    def _():
        pad_rows(wq_s, wq[...], hc)
        do_s[:, :, hc:] = jnp.zeros((2, RQ, do_s.shape[2] - hc), bf16)
        for acc in (g_a, gr_a, sm_a):
            acc[...] = jnp.zeros(acc.shape, f32)

    key_s[pl.ds(pl.multiple_of(c * rm, 64), rm), :] = mem[0]
    key_s[pl.ds(pl.multiple_of((1 - c) * rm, 64), rm), :] = mem_o[0]
    key_s[pl.ds(pl.multiple_of(M + c * rh, 64), rh), :] = hid[0]
    key_s[pl.ds(pl.multiple_of(M + (1 - c) * rh, 64), rh), :] = hid_o[0]

    flip = (iota((RQ, RQ), 0) + iota((RQ, RQ), 1) == RQ - 1).astype(bf16)
    seg_row = segs[pl.ds(s, 1), :]
    own_seg = jnp.where(c == 0, seg_row[:, M : M + RQ], seg_row[:, M + RQ :])
    seg_col = dot(flip, row_to_col(own_seg.astype(f32), RQ).astype(bf16)).astype(jnp.int32)

    rr = RQ // n_t
    for k in range(n_t):
        rows = pl.ds(pl.multiple_of((t_me ^ k) * rr, rr), rr)
        for a in range(2):
            do_s[a, rows, :hc] = datt[k][:, a * hc : (a + 1) * hc]
    for a, x_ref in enumerate((hid, qry)):
        x_rev = dot(flip, x_ref[0]).astype(bf16)
        x_s[a] = x_rev
        q_raw = dot_nt(x_rev, wq_s[...])
        word_s[a] = (q_raw + bw[...]).astype(bf16)
        rel_s[a] = (q_raw + br[...]).astype(bf16)
        qs_s[a] = q_raw + bs[...]

    scale = 1.0 / math.sqrt(DH)
    zero_b = jnp.zeros((), bf16)
    dk_t, dv_t = [None, None], [None, None]
    lane = iota((RQ, LANES), 1)
    first_head = head_mask(0, (RQ, LANES))
    for h in range(3):
        pair = h // 2
        cols = slice(pair * LANES, (pair + 1) * LANES)
        mask2 = head_mask(h, (2 * RQ, LANES))
        kcols = slice(0, 2 * LANES) if h < 2 else slice(2 * LANES, 3 * LANES)
        base = 0 if h < 2 else 64
        own = lane - base == seg_col
        rest = (lane >= base) & (lane < base + 4) & (~own)

        def merge(dst, a, new):
            if h == 0:
                dst[a, :, cols] = new
            elif h == 1:
                dst[a, :, cols] = jnp.where(first_head, dst[a, :, cols], new)
            else:
                dst[a, :, cols] = jnp.where(first_head, new, 0.0)

        def stream(a):
            do_h = jnp.where(head_mask(h, (RQ, LANES)), do_s[a, :, cols], zero_b)
            do_r = (dot(flip, do_h) * scale).astype(bf16)
            pf = dot(flip, p_in[0, h, a])
            dp = dot_nt(do_r, v[0, :, cols])
            t = pf * dp
            delta = jnp.sum(t, -1, keepdims=True)
            ds = t - pf * delta
            ds_s[a] = ds.astype(bf16)
            for half, u0 in enumerate((0, HB)):
                blk = jnp.concatenate([ds[u0 : u0 + HB], jnp.zeros((HB, WB - KT), f32)], 1)
                sk_s[half, a] = pltpu.roll(blk, 1, 1, stride=1, stride_axis=0).astype(bf16)
            dqx = dot(ds_s[a], kx[0, :, kcols])
            side = dqx[:, LANES:] if h < 2 else dqx
            d0 = jnp.sum(jnp.where(own, side, 0.0), -1, keepdims=True)
            d1 = jnp.sum(jnp.where(rest, side, 0.0), -1, keepdims=True)
            merge(dw_s, a, dqx[:, :LANES])
            merge(dg_s, a, d0 * se[0:1, cols] + d1 * se[1:2, cols])
            qs = jnp.where(head_mask(h, (RQ, LANES)), qs_s[a, :, cols], 0.0)
            sm_a[3:4, cols] += jnp.sum(d0 * qs, 0, keepdims=True)
            sm_a[4:5, cols] += jnp.sum(d1 * qs, 0, keepdims=True)

        for a in range(2):
            stream(a)
        for half, u0 in enumerate((0, HB)):
            sk = sk_s[half].reshape(2 * HB, WB)
            dr = dot(sk, rk[u0 : u0 + WB, cols])
            for a in range(2):
                new = dr[a * HB : (a + 1) * HB]
                old = dr_s[a, u0 : u0 + HB, cols] if h == 1 else 0.0
                if h > 0:
                    hm = first_head[:HB]
                    new = jnp.where(hm, old, new) if h == 1 else jnp.where(hm, new, old)
                dr_s[a, u0 : u0 + HB, cols] = new
            r_h = jnp.concatenate([rel_s[a, u0 : u0 + HB, cols] for a in range(2)], 0)
            r_h = jnp.where(head_mask(h, r_h.shape), r_h, zero_b)
            gr_a[cols, u0 : u0 + WB] += dot_tn(r_h, sk)
        w_h = jnp.where(mask2, word_s[:, :, cols].reshape(2 * RQ, LANES), zero_b)
        part = dot_tn(w_h, ds_s[...].reshape(2 * RQ, KT))
        dk_t[pair] = part if dk_t[pair] is None else dk_t[pair] + part
        o_h = jnp.where(mask2, do_s[:, :, cols].reshape(2 * RQ, LANES), zero_b)
        part = dot_tn(o_h, p_in[0, h].reshape(2 * RQ, KT))
        dv_t[pair] = part if dv_t[pair] is None else dv_t[pair] + part

    for row, g in enumerate((dw_s, dr_s, dg_s)):
        sm_a[row : row + 1, :] += jnp.sum(g[0], 0, keepdims=True) + jnp.sum(g[1], 0, keepdims=True)
    for a in range(2):
        dq = (dw_s[a] + dr_s[a] + dg_s[a]).astype(bf16)
        g_a[0] += dot_tn(dq, x_s[a])
        do_s[a, :, :] = dot(flip, dq).astype(bf16)
    share_rows(dq_out, lambda a, rows: do_s[a, rows, :hc], t_me)
    do_s[:, :, hc:] = jnp.zeros((2, RQ, do_s.shape[2] - hc), bf16)

    for i, parts in enumerate((dk_t, dv_t)):
        g_t = jnp.concatenate(parts, 0)
        g_a[1 + i] += dot(g_t.astype(bf16), key_s[...])
        dkv_s[i] = jnp.transpose(g_t[:, M:]).astype(bf16)
    for dst, core in ((dkv_own, c), (dkv_oth, 1 - c)):
        for k in range(n_t):
            rows = pl.ds(pl.multiple_of(core * RQ + (t_me ^ k) * rr, rr), rr)
            dst[k] = jnp.concatenate([dkv_s[0, rows, :hc], dkv_s[1, rows, :hc]], 1)

    @pl.when(step == pl.num_programs(0) - 1)
    def _():
        gr = dot(gr_a[...].astype(bf16), table[...])
        for i in range(2):
            rows = slice(i * hc, (i + 1) * hc)
            last = g_a[2, :hc] if i == 0 else gr[:hc]
            first = g_a[i, :hc]
            gw_own[rows, :] = jnp.where(c == 0, first, last).astype(bf16)
            gw_oth[rows, :] = jnp.where(c == 0, last, first).astype(bf16)
        hi = sm_a[...].astype(bf16)
        lo = (sm_a[...] - hi.astype(f32)).astype(bf16)
        sums = jnp.concatenate([hi, lo], 0)
        for dst in (gw_own, gw_oth):
            dst[2 * hc :, : 2 * LANES] = sums
            dst[2 * hc :, 2 * LANES :] = jnp.zeros((SUM_ROWS, D - 2 * LANES), bf16)


def attn_bwd(meta, p, datt, kx, v, hid, qry, mem, hid_o, mem_o, segs, wq, rk, table, bw, br, bs, se):
    _, rh, _ = hid.shape
    count = p.shape[0]
    rm = mem.shape[1]
    hc = wq.shape[0]
    n_t = len(datt)
    rr = rh // n_t
    sds = jax.ShapeDtypeStruct
    g_shape = (2 * hc + SUM_ROWS, D)
    lanes = by_lane((rr, 2 * hc))
    both = pl.BlockSpec((n_t, rr, 2 * hc), lambda s, *_: (0, 0, s))
    grid_spec = pltpu.PrefetchScalarGridSpec(
        num_scalar_prefetch=1,
        grid=(count,),
        in_specs=[
            per_seq((1, 3, 2, rh, KT)), per_seq((1, KT, 3 * LANES)), per_seq((1, KT, 2 * LANES)),
            from_seq((1, rh, D)), from_seq((1, rh, D)), from_seq((1, rm, D)), from_seq((1, rh, D)), from_seq((1, rm, D)),
            whole(segs.shape), whole(wq.shape), whole(rk.shape), whole(table.shape),
            whole(bw.shape), whole(br.shape), whole(bs.shape), whole(se.shape),
        ] + [lanes] * n_t,
        out_specs=[lanes] * n_t + [both, both, whole(g_shape), whole(g_shape)],
        scratch_shapes=[
            pltpu.VMEM((2 * LANES, D), bf16), pltpu.VMEM((KT, D), bf16), pltpu.VMEM((2, RQ, 2 * LANES), bf16),
            pltpu.VMEM((2, RQ, D), bf16), pltpu.VMEM((2, RQ, 2 * LANES), bf16), pltpu.VMEM((2, RQ, 2 * LANES), bf16),
            pltpu.VMEM((2, RQ, 2 * LANES), f32), pltpu.VMEM((2, RQ, KT), bf16), pltpu.VMEM((2, 2, HB, WB), bf16),
            pltpu.VMEM((2, L, 2 * LANES), bf16), pltpu.VMEM((2, RQ, 2 * LANES), f32), pltpu.VMEM((2, RQ, 2 * LANES), f32),
            pltpu.VMEM((2, RQ, 2 * LANES), f32),
            pltpu.VMEM((3, 2 * LANES, D), f32), pltpu.VMEM((2 * LANES, WIN), f32), pltpu.VMEM((8, 2 * LANES), f32),
        ],
    )
    out = pl.pallas_call(
        attn_bwd_kernel,
        grid_spec=grid_spec,
        out_shape=[sds((rr, count * 2 * hc), bf16)] * n_t + [sds((n_t, rr, count * 2 * hc), bf16)] * 2
        + [sds(g_shape, bf16)] * 2,
        compiler_params=pltpu.CompilerParams(vmem_limit_bytes=58 << 20),
        cost_estimate=pl.CostEstimate(flops=count * 10**10, bytes_accessed=count * 16 * 10**6, transcendentals=0),
        name="attn_bwd",
    )(meta, p, kx, v, hid, qry, mem, hid_o, mem_o, segs, wq, rk, table, bw, br, bs, se, *datt)
    return out[:n_t], out[n_t], out[n_t + 1], out[n_t + 2 :]


def norm_bwd(d_out, scaled, inv_std, gain):
    e = d_out * gain
    return inv_std * (e - jnp.mean(e, -1, keepdims=True) - scaled * jnp.mean(e * scaled, -1, keepdims=True))


def norm_fwd(resid):
    cen = resid - jnp.mean(resid, -1, keepdims=True)
    inv_std = lax.rsqrt(jnp.mean(cen * cen, -1, keepdims=True) + EPS)
    return cen * inv_std, inv_std


GELU_A = 0.7978845608028654
GELU_B = 0.044715


def ffn_kernel(ti, *refs):
    n_t = (len(refs) - 47) // 4
    it = iter(refs)
    take = lambda n: [next(it) for _ in range(n)]
    att = [take(n_t) for _ in range(2)]
    (hid, qry, cot_h, cot_q, wi_own, wo_own, wx_own, wgot, n1g, n1b, bo, n2g, n2b) = take(13)
    datt_out = [take(n_t) for _ in range(2)]
    big_out = take(9)
    vec_out, gb_out = take(2)
    (wi, wo, wx, n1_s, sc1_s, inv1_s, gp_s, acc_s, dres2_s, x_s) = take(10)
    big = take(9)
    (out_h, out_q, dres_out, inner_out, act_out, dpre_out, dout_out, dattn_out, attr_out) = big
    sems, sems_x, sems_o, sems_k = take(4)
    t_me = ti[0]
    hc = attr_out.shape[2]
    rows = dres_out.shape[0]
    half = rows // 2
    n_p = wgot.shape[0]
    parts = ((wx, wx_own), (wi, wi_own), (wo, wo_own))

    def piece_copy(i, k, j):
        dst = parts[i][0]
        count = dst.shape[1] // n_p
        start = ((wi.shape[1] + wo.shape[1]) // n_p, 0, wi.shape[1] // n_p)[i]
        return pltpu.make_async_copy(
            wgot.at[j, k - 1, pl.ds(start, count), :], dst.at[k, pl.ds(j * count, count), :], sems.at[i, k, j]
        )

    copies = []
    for i, (dst, own) in enumerate(parts):
        group = [[pltpu.make_async_copy(own, dst.at[0], sems.at[i, 0, 0])]]
        group += [[piece_copy(i, k, j) for j in range(n_p)] for k in range(1, n_t)]
        copies.append(group)
    rr = x_s.shape[2]
    mine = [
        pltpu.make_async_copy(x.at[:, pl.ds(t_me * rr, rr), :], x_s.at[i], sems_x.at[i])
        for i, x in enumerate((hid, qry, cot_h, cot_q))
    ]
    for copy in mine[:2]:
        copy.start()
    for per_k in copies[0]:
        for copy in per_k:
            copy.start()
    for k in range(n_t):
        for copy in copies[1][k] + copies[2][k]:
            copy.start()
    for copy in mine[2:]:
        copy.start()
    leave = [pltpu.make_async_copy(big[i], big_out[i], sems_o.at[i]) for i in range(9)]
    leave_k = lambda i, k: pltpu.make_async_copy(big[4 + i].at[k], big_out[4 + i].at[k], sems_k.at[i, k])

    halves = (slice(0, half), slice(half, rows))
    for per_k in copies[0]:
        for copy in per_k:
            copy.wait()
    n_h = half // (2 * rr)
    for a in range(2):
        r = halves[a]
        mine[a].wait()
        acc = x_s[a].reshape(half, D).astype(f32)
        for k in range(n_t):
            pieces = [
                att[i][k][:, (2 * s + a) * hc : (2 * s + a + 1) * hc] for i in range(2) for s in range(n_h)
            ]
            part = jnp.concatenate(pieces, 0)
            attr_out[k, r, :] = part
            acc = acc + dot(part, wx[k, :hc, :])
        scaled, inv_std = norm_fwd(acc)
        sc1_s[r, :] = scaled
        inv1_s[r, :] = jnp.broadcast_to(inv_std, (half, LANES))
        n1 = scaled * n1g[...] + n1b[...]
        n1_s[r, :] = n1
        inner_out[r, :] = n1.astype(bf16)
    leave[8].start()
    leave[3].start()
    acc_s[...] = jnp.zeros(acc_s.shape, f32)

    def up(k, carry):
        @pl.when(k == 0)
        def _():
            copies[1][0][0].wait()
            copies[2][0][0].wait()

        @pl.when(k > 0)
        def _():
            for i in (1, 2):
                for j in range(n_p):
                    piece_copy(i, k, j).wait()

        bias = wx[k, hc : hc + 1, :].astype(f32) + wx[k, hc + 1 : hc + 2, :].astype(f32)
        for r in halves:
            pre = dot(inner_out[r, :], wi[k]) + bias
            sq = pre * pre
            th = jnp.tanh(GELU_A * (pre + GELU_B * (pre * sq)))
            act_out[k, r, :] = (0.5 * pre * (1.0 + th)).astype(bf16)
            gp_s[k, r, :] = 0.5 * (1.0 + th) + (0.5 * pre) * (1.0 - th * th) * (GELU_A + (3.0 * GELU_A * GELU_B) * sq)
            acc_s[r, :] += dot(act_out[k, r, :], wo[k])
        leave_k(0, k).start()
        return carry

    lax.fori_loop(0, n_t, up, 0)

    sums = [None] * 3
    for a, o_ref in enumerate((out_h, out_q)):
        r = halves[a]
        scaled, inv_std = norm_fwd(n1_s[r, :] + (acc_s[r, :] + bo[...]))
        o_ref[...] = scaled * n2g[...] + n2b[...]
        leave[a].start()
        mine[2 + a].wait()
        cot = x_s[2 + a].reshape(half, D).astype(f32)
        d2 = norm_bwd(cot, scaled, inv_std, n2g[...])
        dres2_s[r, :] = d2
        dout_out[r, :] = d2.astype(bf16)
        for i, g in enumerate((cot * scaled, cot, d2)):
            g = jnp.sum(g, 0, keepdims=True)
            sums[i] = g if a == 0 else sums[i] + g
    leave[6].start()
    vec_out[2:3, :] = sums[0]
    vec_out[3:4, :] = sums[1]
    vec_out[4:5, :] = sums[2]
    acc_s[...] = jnp.zeros(acc_s.shape, f32)

    def down(k, carry):
        total = None
        for r in halves:
            d_pre = dot_nt(dout_out[r, :], wo[k]) * gp_s[k, r, :]
            g = jnp.sum(d_pre, 0, keepdims=True)
            total = g if total is None else total + g
            dpre_out[k, r, :] = d_pre.astype(bf16)
            acc_s[r, :] += dot_nt(dpre_out[k, r, :], wi[k])
        gb_out[pl.ds(k, 1), :] = total
        leave_k(1, k).start()
        return carry

    lax.fori_loop(0, n_t, down, 0)
    for a in range(2):
        r = halves[a]
        d_n1 = dres2_s[r, :] + acc_s[r, :]
        scaled = sc1_s[r, :]
        for i, g in enumerate((d_n1 * scaled, d_n1)):
            g = jnp.sum(g, 0, keepdims=True)
            vec_out[i : i + 1, :] = g if a == 0 else vec_out[i : i + 1, :] + g
        d1 = norm_bwd(d_n1, scaled, inv1_s[r, :1], n1g[...])
        dres_out[r, :] = d1
        dattn_out[r, :] = d1.astype(bf16)
    leave[2].start()
    leave[7].start()
    for k in range(n_t):
        part = dot_nt(dattn_out[...], wx[k, :hc, :]).astype(bf16)
        for i in range(2):
            for s in range(n_h):
                first = (i * n_h + s) * rr
                datt_out[i][k][:, 2 * s * hc : (2 * s + 2) * hc] = jnp.concatenate(
                    [part[first : first + rr], part[half + first : half + first + rr]], 1
                )
    for i in (0, 1, 2, 3, 6, 7, 8):
        leave[i].wait()
    for i in range(2):
        for k in range(n_t):
            leave_k(i, k).wait()


def ffn(ti, att0, att1, hid, qry, cot_h, cot_q, w_inner, w_outer, wx_own, wgot, n1g, n1b, bo, n2g, n2b, hc):
    n_t = len(att0)
    n_f = w_outer.shape[0]
    n_s, rr = hid.shape[0], hid.shape[1] // n_t
    half = n_s * rr
    rows = 2 * half
    sds = jax.ShapeDtypeStruct
    vm = pl.BlockSpec(memory_space=pltpu.VMEM)
    hbm = pl.BlockSpec(memory_space=pl.ANY)
    big = [
        ((half, D), f32), ((half, D), f32), ((rows, D), f32), ((rows, D), bf16), ((n_t, rows, n_f), bf16),
        ((n_t, rows, n_f), bf16), ((rows, D), bf16), ((rows, D), bf16), ((n_t, rows, hc), bf16),
    ]
    out = pl.pallas_call(
        ffn_kernel,
        in_specs=[pl.BlockSpec(memory_space=pltpu.SMEM)] + [vm] * (2 * n_t) + [hbm] * 8 + [vm] * 5,
        out_specs=[vm] * (2 * n_t) + [hbm] * len(big) + [vm] * 2,
        out_shape=[sds(att0[0].shape, bf16)] * (2 * n_t) + [sds(*b) for b in big] + [sds((5, D), f32), sds((n_t, n_f), f32)],
        scratch_shapes=[
            pltpu.VMEM((n_t,) + w_inner.shape, bf16), pltpu.VMEM((n_t,) + w_outer.shape, bf16),
            pltpu.VMEM((n_t,) + wx_own.shape, bf16),
            pltpu.VMEM((rows, D), f32), pltpu.VMEM((rows, D), f32), pltpu.VMEM((rows, LANES), f32),
            pltpu.VMEM((n_t, rows, n_f), f32), pltpu.VMEM((rows, D), f32), pltpu.VMEM((rows, D), f32),
            pltpu.VMEM((4, n_s, rr, D), bf16),
        ] + [pltpu.VMEM(*b) for b in big] + [
            pltpu.SemaphoreType.DMA((3, n_t, wgot.shape[0])), pltpu.SemaphoreType.DMA((4,)),
            pltpu.SemaphoreType.DMA((len(big),)), pltpu.SemaphoreType.DMA((2, n_t)),
        ],
        compiler_params=pltpu.CompilerParams(vmem_limit_bytes=60 << 20),
        cost_estimate=pl.CostEstimate(flops=20 * 10**9, bytes_accessed=25 * 10**6, transcendentals=2 * 10**6),
        name="ffn",
    )(ti, *att0, *att1, hid, qry, cot_h, cot_q, w_inner, w_outer, wx_own, wgot, n1g, n1b, bo, n2g, n2b)
    return out[:n_t], out[n_t : 2 * n_t], out[2 * n_t : 2 * n_t + 9], out[2 * n_t + 9 :]


XROWS = 256


def wgrad_kernel(pos, inner, act, dpre, dout, attr, dattn, vec, gb, ga_out, own_out, oth_out, gx_s):
    hc = attr.shape[2]
    n_p = ga_out.shape[0]
    d, c = pos[0], pos[1]
    k = pl.program_id(0)
    z = pos[2] ^ k
    n_i, n_o, n_x = D // n_p, act.shape[2] // n_p, XROWS // n_p
    gx_s[:hc, :] = dot_tn(attr[0], dattn[...])
    gx_s[hc:, :] = jnp.zeros((gx_s.shape[0] - hc, D), f32)
    gx_s[hc : hc + 1, :] = gb[pl.ds(k, 1), :]
    for t in range(D // hc):
        @pl.when(z == t)
        def _():
            gx_s[hc + 8 : hc + 13, :hc] = vec[:, t * hc : (t + 1) * hc]
    n_a = ga_out.shape[2] - n_i
    g = dot_tn(inner[...], dpre[0]).astype(bf16)
    for j in range(n_p):
        ga_out[j, 0, :n_i] = g[j * n_i : (j + 1) * n_i]
    g = dot_tn(act[0], dout[...])
    for j in range(n_p):
        ga_out[j, 0, n_i:] = g[j * n_o : j * n_o + n_a].astype(bf16)
    for m in range(n_p // 2):
        halves = [
            jnp.concatenate([g[j * n_o + n_a : (j + 1) * n_o], gx_s[j * n_x : (j + 1) * n_x]], 0)
            for j in (2 * m, 2 * m + 1)
        ]
        own_out[m ^ d, 0] = jnp.where(c == 0, halves[0], halves[1]).astype(bf16)
        oth_out[m ^ d, 0] = jnp.where(c == 0, halves[1], halves[0]).astype(bf16)


def wgrad(pos, inner, act, dpre, dout, attr, dattn, vec, gb, n_d):
    n_t, rows, n_f = act.shape
    n_p = 2 * n_d
    n_o = n_f // n_p
    n_a = 2 * n_o // 3
    first = D // n_p + n_a
    rest = n_o - n_a + XROWS // n_p
    return pl.pallas_call(
        wgrad_kernel,
        grid=(n_t,),
        in_specs=[
            pl.BlockSpec(memory_space=pltpu.SMEM),
            whole(inner.shape), per_seq((1, rows, n_f)), per_seq((1, rows, n_f)), whole(dout.shape),
            per_seq((1,) + attr.shape[1:]), whole(dattn.shape), whole(vec.shape), whole(gb.shape),
        ],
        out_specs=[per_seq((n_p, 1, first, D), 1)] + [per_seq((n_d, 1, rest, D), 1)] * 2,
        out_shape=[
            jax.ShapeDtypeStruct((n_p, n_t, first, D), bf16)
        ] + [jax.ShapeDtypeStruct((n_d, n_t, rest, D), bf16)] * 2,
        scratch_shapes=[pltpu.VMEM((XROWS, D), f32)],
        compiler_params=pltpu.CompilerParams(vmem_limit_bytes=60 << 20),
        cost_estimate=pl.CostEstimate(flops=6 * 10**9, bytes_accessed=20 * 10**6, transcendentals=0),
        name="wgrad",
    )(pos, inner, act, dpre, dout, attr, dattn, vec, gb)


def final_kernel(*refs):
    n_t = (len(refs) - 7) // 2
    rows = (refs[:n_t], refs[n_t : 2 * n_t])
    w_own, wgot, dres, gh, gq, w_s, sems = refs[2 * n_t :]
    n_p = wgot.shape[0]
    half = gh.shape[0]
    rr = rows[0][0].shape[0] // 2
    n_h = half // (2 * rr)
    hc = rows[0][0].shape[1] // (2 * n_h)
    count = wgot.shape[2]
    copies = [[pltpu.make_async_copy(w_own, w_s.at[0], sems.at[0, 0])]]
    for k in range(1, n_t):
        copies.append([
            pltpu.make_async_copy(wgot.at[j, k - 1], w_s.at[k, pl.ds(j * count, count), :], sems.at[k, j])
            for j in range(n_p)
        ])
    for per_k in copies:
        for copy in per_k:
            copy.start()
    gh[...] = dres[:half, :]
    gq[...] = dres[half:, :]
    for k in range(n_t):
        for copy in copies[k]:
            copy.wait()
        wq, wk, wv = (w_s[k, i * hc : (i + 1) * hc, :] for i in range(3))

        def kind(low, i):
            return jnp.concatenate([
                rows[side][k][low : low + rr, (2 * s + i) * hc : (2 * s + i + 1) * hc]
                for side in range(2) for s in range(n_h)
            ], 0)

        gh[...] += dot(kind(0, 0), wq) + dot(kind(rr, 0), wk) + dot(kind(rr, 1), wv)
        gq[...] += dot(kind(0, 1), wq)


def final_proj(rows0, rows1, w_own, wgot, dres):
    half = dres.shape[0] // 2
    n_t = len(rows0)
    vm = pl.BlockSpec(memory_space=pltpu.VMEM)
    hbm = pl.BlockSpec(memory_space=pl.ANY)
    return pl.pallas_call(
        final_kernel,
        in_specs=[vm] * (2 * n_t) + [hbm, hbm, vm],
        out_shape=[jax.ShapeDtypeStruct((half, D), f32)] * 2,
        scratch_shapes=[pltpu.VMEM((n_t,) + w_own.shape, bf16), pltpu.SemaphoreType.DMA((n_t, wgot.shape[0]))],
        compiler_params=pltpu.CompilerParams(vmem_limit_bytes=48 << 20),
        cost_estimate=pl.CostEstimate(flops=2 * 10**9, bytes_accessed=8 * 10**6, transcendentals=0),
        name="final_proj",
    )(*rows0, *rows1, w_own, wgot, dres)


def unpack_kernel(pos, own, oth, gi, go, gx, gi_s, go_s, gx_s, sems):
    d, c = pos[0], pos[1]
    n_d = own.shape[0]
    n_p = 2 * n_d
    n_i, n_o, n_x = gi_s.shape[0] // n_p, go_s.shape[0] // n_p, gx_s.shape[0] // n_p
    copies = []
    for j in range(n_p):
        m = d ^ (j // 2)
        piece = jnp.where(c == j % 2, own[m].astype(f32), oth[m].astype(f32))
        parts = ((gi_s, gi, n_i, 0), (go_s, go, n_o, n_i), (gx_s, gx, n_x, n_i + n_o))
        for i, (src, dst, count, first) in enumerate(parts):
            rows = slice(j * count, (j + 1) * count)
            src[rows, :] = piece[first : first + count]
            copies.append(pltpu.make_async_copy(src.at[rows, :], dst.at[rows, :], sems.at[i, j]))
            copies[-1].start()
    for copy in copies:
        copy.wait()


def unpack(pos, own, oth, n_f):
    vm = pl.BlockSpec(memory_space=pltpu.VMEM)
    hbm = pl.BlockSpec(memory_space=pl.ANY)
    shapes = [(D, n_f), (n_f, D), (XROWS, D)]
    return pl.pallas_call(
        unpack_kernel,
        in_specs=[pl.BlockSpec(memory_space=pltpu.SMEM), vm, vm],
        out_specs=[hbm] * 3,
        out_shape=[jax.ShapeDtypeStruct(shape, f32) for shape in shapes],
        scratch_shapes=[pltpu.VMEM(shape, f32) for shape in shapes] + [pltpu.SemaphoreType.DMA((3, 2 * own.shape[0]))],
        compiler_params=pltpu.CompilerParams(vmem_limit_bytes=48 << 20),
        name="unpack",
    )(pos, own, oth)


def unpack_heads_kernel(pos, own, oth, gq, gk, gv, gr, sm):
    c = pos[1]
    hc = gq.shape[0]
    for i, g in enumerate((gq, gk, gv, gr)):
        rows = slice((i % 2) * hc, (i % 2 + 1) * hc)
        g[...] = jnp.where(c == i // 2, own[rows, :].astype(f32), oth[rows, :].astype(f32))
    sums = own[2 * hc :, :hc].astype(f32)
    sm[...] = sums[:8] + sums[8:]


def unpack_heads(pos, own, oth, hc):
    vm = pl.BlockSpec(memory_space=pltpu.VMEM)
    sds = jax.ShapeDtypeStruct
    return pl.pallas_call(
        unpack_heads_kernel,
        in_specs=[pl.BlockSpec(memory_space=pltpu.SMEM), vm, vm],
        out_shape=[sds((hc, D), f32)] * 4 + [sds((8, hc), f32)],
        compiler_params=pltpu.CompilerParams(vmem_limit_bytes=48 << 20),
        name="unpack_heads",
    )(pos, own, oth)


def table_rows(start, count):
    step = 32
    freq = 1.0 / 10000.0 ** (jnp.arange(0, D, 2).astype(f32) / D)
    coarse = (M + L - start - step * jnp.arange(count // step)).astype(f32)[:, None] * freq[None]
    fine = jnp.arange(step).astype(f32)[:, None] * freq[None]
    sin_c, cos_c = jnp.sin(coarse)[:, None], jnp.cos(coarse)[:, None]
    sin_f, cos_f = jnp.sin(fine)[None], jnp.cos(fine)[None]
    sin_a = sin_c * cos_f - cos_c * sin_f
    cos_a = cos_c * cos_f + sin_c * sin_f
    return jnp.concatenate([sin_a, cos_a], -1).reshape(count, D).astype(bf16)


def body(
    hidden, query, memory, cot_hidden, cot_query, lengths, ranks, segments,
    w_query, w_key, w_value, w_rel, w_out, bias_word, bias_rel, bias_seg, seg_embed,
    norm1_gain, norm1_bias, w_inner, b_inner, w_outer, b_outer, norm2_gain, norm2_bias,
):
    n_s, rh, _ = hidden.shape
    n_t = lax.axis_size("tensor")
    n_c = lax.axis_size("ctx")
    heads = bias_word.shape[0]
    hc = heads * DH
    n_f = w_inner.shape[1]
    rr = rh // n_t
    ci = lax.axis_index("ctx")
    ti = lax.axis_index("tensor")
    swap = [(i, (i + 1) % n_c) for i in range(n_c)]

    hid_o = lax.ppermute(hidden, "ctx", swap)
    mem_o = lax.ppermute(memory, "ctx", swap)

    n_d = lax.axis_size("dp")
    tile = 16
    di = lax.axis_index("dp")
    n_p = n_d * n_c
    while (D // n_p) % tile or (XROWS // n_p) % tile:
        n_p //= 2
    groups = n_d * n_c // n_p
    piece = (di * n_c + ci) // groups

    def across(x, k):
        return lax.ppermute(x, "tensor", [(i, i ^ k) for i in range(n_t)])

    tie = lax.optimization_barrier

    def send(own):
        return [across(own, k) for k in range(1, n_t)]

    def spread(got):
        return lax.all_gather(jnp.stack(got), ("dp", "ctx"), axis=0, tiled=False)[::groups]

    def cut(x):
        count = x.shape[0] // n_p
        return lax.dynamic_slice_in_dim(x, piece * count, count, 0)

    b_hi = b_inner.astype(bf16)
    b_lo = (b_inner - b_hi.astype(f32)).astype(bf16)
    wx = jnp.concatenate([w_out, b_hi[None], b_lo[None], jnp.zeros((XROWS - hc - 2, n_f), bf16)], 0)
    got = send(jnp.concatenate([cut(w_inner), cut(w_outer), cut(wx)], 0))
    wq, wk, wv, wr = (jnp.swapaxes(w, 0, 1) for w in (w_query, w_key, w_value, w_rel))
    w_t = jnp.concatenate([wq, wk, wv, jnp.zeros((640 - 3 * hc, D), bf16)], 0)
    ti1 = ti[None].astype(jnp.int32)
    pos = jnp.stack([di, ci, ti]).astype(jnp.int32)
    got_t = send(cut(w_t))

    table = table_rows(L - ci * rh - rh, WIN)
    wr_p = jnp.concatenate([wr, jnp.zeros((2 * LANES - hc, D), bf16)], 0)
    rk = lax.dot_general(table, wr_p, (((1,), (1,)), ((), ())), preferred_element_type=f32).astype(bf16)
    row = lambda v: jnp.pad(v.reshape(-1, hc), ((0, 0), (0, 2 * LANES - hc)))
    bw, br, bs, se = row(bias_word), row(bias_rel), row(bias_seg), row(seg_embed)

    half_s = n_s // 2
    metas = [
        jnp.concatenate([ci[None].astype(jnp.int32), lengths, ti1, jnp.full((1,), i * half_s, jnp.int32)]) for i in range(2)
    ]

    def forward(meta):
        return attn_fwd(
            meta, hidden, query, memory, hid_o, mem_o, ranks, segments, wq, wk, wv, rk, bw, br, bs, se, n_t, half_s
        )

    def share(own):
        return [own[0]] + [across(own[k], k) for k in range(1, n_t)]

    def along_dp(x, m):
        return lax.ppermute(x, "dp", [(i, i ^ m) for i in range(n_d)])

    def add(*terms):
        total = terms[0].astype(f32)
        for term in terms[1:]:
            total = total + term.astype(f32)
        return total.astype(bf16)

    def tie_all(*groups):
        flat = tie(tuple(x for group in groups for x in group))
        out, first = [], 0
        for group in groups:
            out.append(list(flat[first : first + len(group)]))
            first += len(group)
        return out

    att0, kept0 = forward(metas[0])
    att0, got = tie_all(att0, got)
    wgot = spread(got)
    att0 = share(att0)
    meta, _ = tie((metas[1], got[0]))
    att1, kept1 = forward(meta)
    att1, att0, got_t = tie_all(att1, att0, got_t)
    att1 = share(att1)
    vec1 = lambda x: x[None]
    got_t[0], _ = tie((got_t[0], wgot[0, 0, :1]))
    wgot_t = spread(got_t)
    datt0, datt1, big, (vec, gb) = ffn(
        ti1, att0, att1, hidden, query, cot_hidden, cot_query, w_inner, w_outer, wx, wgot,
        vec1(norm1_gain), vec1(norm1_bias), vec1(b_outer), vec1(norm2_gain), vec1(norm2_bias), hc,
    )
    out_h, out_q, dres, inner, act, dpre, dout, dattn, attr = big
    datt0 = share(datt0)
    ga, gb_own, gb_oth = wgrad(pos, inner, act, dpre, dout, attr, dattn, vec, gb, n_d)
    datt0, datt1, (ga, gb_oth, wgot_t) = tie_all(datt0, datt1, [ga, gb_oth, wgot_t])
    datt1 = share(datt1)
    gb_got = lax.ppermute(gb_oth, "ctx", swap)
    meta, ga = tie((metas[0], ga))
    ga = lax.psum_scatter(ga, ("dp", "ctx"), scatter_dimension=0, tiled=True)[0]

    def backward(meta, kept, datt):
        p, kx, v = kept
        return attn_bwd(
            meta, p, datt, kx, v, hidden, query, memory, hid_o, mem_o, segments, wq, rk, table, bw, br, bs, se
        )

    def payload(dq, dkv_own, dkv_oth):
        got = lax.ppermute(dkv_oth, "ctx", swap)
        return [jnp.concatenate([dq[k], add(dkv_own[k], got[k])], 0) for k in range(n_t)]

    dq, dkv_own, dkv_oth, gw0 = backward(meta, kept0, datt0)
    (dkv_oth, gb_got), datt1 = tie_all([dkv_oth, gb_got], datt1)
    pay = payload(dq, dkv_own, dkv_oth)
    gb = [add(gb_own[m], gb_got[m]) for m in range(n_d)]
    (meta,), pay, gb = tie_all([metas[1]], pay, gb)
    rows0 = share(pay)
    gb_got = [along_dp(gb[m], m) for m in range(1, n_d)]
    dq, dkv_own, dkv_oth, gw1 = backward(meta, kept1, datt1)
    (dkv_oth, ga), rows0, gw1, gb_got = tie_all([dkv_oth, ga], rows0, gw1, gb_got)

    total = [jnp.concatenate([ga[k], add(gb[0][k], *[g[k] for g in gb_got])], 0) for k in range(n_t)]
    total_got = [across(total[k], k) for k in range(1, n_t)]
    pay = payload(dq, dkv_own, dkv_oth)
    part = add(gw0[0], gw1[0], lax.ppermute(add(gw0[1], gw1[1]), "ctx", swap))
    mask = 1
    while mask < n_d:
        part = add(part, along_dp(part, mask))
        mask *= 2
    (part,), pay, total_got = tie_all([part], pay, total_got)
    total = add(total[0], *total_got)

    pay, (total, part) = tie_all(pay, [total, part])
    rows1 = share(pay)
    others = [along_dp(total, m) for m in range(1, n_d)]
    *gwt, sm = unpack_heads(pos, part, lax.ppermute(part, "ctx", swap), hc)
    gwt = [jnp.swapaxes(g, 0, 1) for g in gwt]
    rows1, others = tie_all(rows1, others)
    pieces = jnp.stack([total] + others)
    grad_h, grad_q = final_proj(rows0, rows1, w_t, wgot_t, dres)
    g_inner, g_outer, g_x = unpack(pos, pieces, lax.ppermute(pieces, "ctx", swap), n_f)
    vecs = g_x[hc + 8 : hc + 13, :hc]
    heads_of = lambda r: r.reshape(heads, DH)
    shape = (n_s, rr, D)
    return (
        out_h.reshape(shape), out_q.reshape(shape), grad_h.reshape(shape), grad_q.reshape(shape),
        gwt[0], gwt[1], gwt[2], gwt[3], g_x[:hc],
        heads_of(sm[0]), heads_of(sm[1]), heads_of(sm[2]), sm[3:5].reshape(2, heads, DH),
        vecs[0], vecs[1], g_inner, g_x[hc], g_outer,
        vecs[4], vecs[2], vecs[3],
    )


def solution(mesh):
    rows = P("dp", "ctx", None)
    by_col = P(None, "tensor")
    by_row = P("tensor", None)
    own_rows = P("dp", ("ctx", "tensor"), None)
    vec = P("tensor")
    return jax.shard_map(
        body,
        mesh=mesh,
        in_specs=(
            rows, rows, rows, rows, rows, P("dp"), P("dp", None), P("dp", None),
            by_col, by_col, by_col, by_col, by_row, by_row, by_row, by_row, P(None, "tensor", None),
            P(), P(), by_col, vec, by_row, P(), P(), P(),
        ),
        out_specs=(
            own_rows, own_rows, own_rows, own_rows,
            by_col, by_col, by_col, by_col, by_row, by_row, by_row, by_row, P(None, "tensor", None),
            vec, vec, by_col, vec, by_row, vec, vec, vec,
        ),
        check_vma=False,
    )
```

profile of v0, /device:TPU:9, one launch (start us, length us, event | category | flops | bytes accessed | tf_op | source)
XLA Modules:
  0.0 306.5 jit_solution(9787827891706836211)
XLA Ops:
  11.3 2.5 collective-permute-start.3
  19.2 2.4 convolution_convert_fusion.rk
  21.6 22.5 %attn_fwd.2 = (bf16[64,768]{1,0:T(8,128)(2,1)}, bf16[64,768]{1,0:T(8,128)(2,1)}, bf16[64,768]{1,0:T(8,128)(2,1)}, bf16[64,768]{1,0:T(8,128)(2,1)}, bf16[2,3,2,25...) custom-call(s32[7]{0:T(128)} %get-tuple-element.210.meta, ...), custom_call_target="tpu_custom_call" | custom-call | flops 20000000000 | bytes 32000000 | tf_op jit(solution)/shard_map/attn_fwd/pallas_call | solution.py:216
  48.7 2.4 collective-permute-start.9
  55.7 22.6 %attn_fwd.3 = (bf16[64,768]{1,0:T(8,128)(2,1)}, bf16[64,768]{1,0:T(8,128)(2,1)}, bf16[64,768]{1,0:T(8,128)(2,1)}, bf16[64,768]{1,0:T(8,128)(2,1)}, bf16[2,3,2,25...) custom-call(s32[7]{0:T(128)} %pad_add_fusion.meta, bf16[4,256,768]{2,1,0:T(8,128)(2,1)} %hid.7, ...), custom_call_target="tpu_custom_call" | custom-call | flops 20000000000 | bytes 32000000 | tf_op jit(solution)/shard_map/attn_fwd/pallas_call | solution.py:216
  82.8 2.6 collective-permute-start.11
  88.0 3.3 %collective-permute-done.12.refs_6_ = bf16[64,768]{1,0:T(8,128)(2,1)S(1)} collective-permute-done((bf16[64,768]{1,0:T(8,128)(2,1)}, bf16[64,768]{1,0:T(8,128)(2,1)S(1)}, u32[]{:S(2)}, u32[]{:S(2)}) %collective-permute-start.12) | collective-permute-done | bytes 98336 | tf_op jit(solution)/shard_map/ppermute | solution.py:838
  91.3 3.9 %collective-permute-done.13.refs_7_ = bf16[64,768]{1,0:T(8,128)(2,1)S(1)} collective-permute-done((bf16[64,768]{1,0:T(8,128)(2,1)}, bf16[64,768]{1,0:T(8,128)(2,1)S(1)}, u32[]{:S(2)}, u32[]{:S(2)}) %collective-permute-start.13) | collective-permute-done | bytes 98336 | tf_op jit(solution)/shard_map/ppermute | solution.py:838
  95.2 6.0 %all-gather.5.cloned.1.call-done = bf16[24,224,768]{2,1,0:T(8,128)(2,1)} async-done(((bf16[3,224,768]{2,1,0:T(8,128)(2,1)}), bf16[24,224,768]{2,1,0:T(8,128)(2,1)}) %all-gather.5.cloned.1.call-update) | async-done | bytes 8257552 | tf_op jit(solution)/shard_map/all_gather | solution.py:846
  101.2 28.2 %ffn.1 = (bf16[64,768]{1,0:T(8,128)(2,1)}, bf16[64,768]{1,0:T(8,128)(2,1)}, bf16[64,768]{1,0:T(8,128)(2,1)}, bf16[64,768]{1,0:T(8,128)(2,1)}, bf16[64,768]{1,0:T...) custom-call(s32[1]{0:T(128)} %bitcast.ti, ...), custom_call_target="tpu_custom_call" | custom-call | flops 20000000000 | bytes 25000000 | tf_op jit(solution)/shard_map/ffn/pallas_call | solution.py:608
  132.1 12.1 %wgrad.1 = (bf16[8,4,160,768]{3,2,1,0:T(8,128)(2,1)}, bf16[4,4,64,768]{3,2,1,0:T(8,128)(2,1)}, bf16[4,4,64,768]{3,2,1,0:T(8,128)(2,1)}) custom-call(s32[3]{0:T(128)} %pad_add_fusion.3.pos, bf16[512,768]{1,0:T(8,128)(2,1)} %get-tuple-element.196.inner, bf16[4,512,768]{2,1,0:T(8,128)(2,1)} %get-tuple-element.197.act, ...), custom_call_target="tpu_custom_call" | custom-call | flops 6000000000 | bytes 20000000 | tf_op jit(solution)/shard_map/wgrad/pallas_call | solution.py:670
  151.4 24.9 %attn_bwd.2 = (bf16[64,768]{1,0:T(8,128)(2,1)}, bf16[64,768]{1,0:T(8,128)(2,1)}, bf16[64,768]{1,0:T(8,128)(2,1)}, bf16[64,768]{1,0:T(8,128)(2,1)}, bf16[4,64,768...) custom-call(s32[7]{0:T(128)} %get-tuple-element.210.meta, ...), custom_call_target="tpu_custom_call" | custom-call | flops 20000000000 | bytes 32000000 | tf_op jit(solution)/shard_map/attn_bwd/pallas_call | solution.py:406
  179.0 2.2 collective-permute-start.22
  184.6 4.1 %collective-permute-done.22.refs_1_ = bf16[128,768]{1,0:T(8,128)(2,1)S(1)} collective-permute-done((bf16[128,768]{1,0:T(8,128)(2,1)S(1)}, bf16[128,768]{1,0:T(8,128)(2,1)S(1)}, u32[]{:S(2)}, u32[]{:S(2)}) %collective-permute-start.22) | collective-permute-done | bytes 196640 | tf_op jit(solution)/shard_map/ppermute | solution.py:838
  189.8 24.5 %attn_bwd.3 = (bf16[64,768]{1,0:T(8,128)(2,1)}, bf16[64,768]{1,0:T(8,128)(2,1)}, bf16[64,768]{1,0:T(8,128)(2,1)}, bf16[64,768]{1,0:T(8,128)(2,1)}, bf16[4,64,768...) custom-call(s32[7]{0:T(128)} %pad_add_fusion.meta, ...), custom_call_target="tpu_custom_call" | custom-call | flops 20000000000 | bytes 32000000 | tf_op jit(solution)/shard_map/attn_bwd/pallas_call | solution.py:406
  215.1 9.1 %reduce-scatter.2.cloned.1.call-done = bf16[1,4,160,768]{3,2,1,0:T(8,128)(2,1)} async-done(((bf16[8,4,160,768]{3,2,1,0:T(8,128)(2,1)}), bf16[1,4,160,768]{3,2,1,0:T(8,128)(2,1)}) %reduce-scatter.2.cloned.1.call-update) | async-done | bytes 983056 | tf_op jit(solution)/shard_map/reduce_scatter | solution.py:920
  231.6 11.5 %collective-permute-done.29 = bf16[400,768]{1,0:T(8,128)(2,1)S(1)} collective-permute-done((bf16[400,768]{1,0:T(8,128)(2,1)S(1)}, bf16[400,768]{1,0:T(8,128)(2,1)S(1)}, u32[]{:S(2)}, u32[]{:S(2)}) %collective-permute-start.29) | collective-permute-done | bytes 614432 | tf_op jit(solution)/shard_map/ppermute | solution.py:882
  244.2 13.3 %collective-permute-done.30 = bf16[400,768]{1,0:T(8,128)(2,1)S(1)} collective-permute-done((bf16[400,768]{1,0:T(8,128)(2,1)S(1)}, bf16[400,768]{1,0:T(8,128)(2,1)S(1)}, u32[]{:S(2)}, u32[]{:S(2)}) %collective-permute-start.30) | collective-permute-done | bytes 614432 | tf_op jit(solution)/shard_map/ppermute | solution.py:882
  257.7 3.4 %collective-permute-done.34 = bf16[224,768]{1,0:T(8,128)(2,1)S(1)} collective-permute-done((bf16[224,768]{1,0:T(8,128)(2,1)S(1)}, bf16[224,768]{1,0:T(8,128)(2,1)S(1)}, u32[]{:S(2)}, u32[]{:S(2)}) %collective-permute-start.34) | collective-permute-done | bytes 344096 | tf_op jit(solution)/shard_map/ppermute | solution.py:838
  264.1 2.3 collective-permute-start.36
  267.1 11.8 %collective-permute-done.36.refs_6_ = bf16[128,768]{1,0:T(8,128)(2,1)S(1)} collective-permute-done((bf16[128,768]{1,0:T(8,128)(2,1)S(1)}, bf16[128,768]{1,0:T(8,128)(2,1)S(1)}, u32[]{:S(2)}, u32[]{:S(2)}) %collective-permute-start.36) | collective-permute-done | bytes 196640 | tf_op jit(solution)/shard_map/ppermute | solution.py:838
  278.9 4.2 %collective-permute-done.37.refs_7_ = bf16[128,768]{1,0:T(8,128)(2,1)S(1)} collective-permute-done((bf16[128,768]{1,0:T(8,128)(2,1)S(1)}, bf16[128,768]{1,0:T(8,128)(2,1)S(1)}, u32[]{:S(2)}, u32[]{:S(2)}) %collective-permute-start.37) | collective-permute-done | bytes 196640 | tf_op jit(solution)/shard_map/ppermute | solution.py:838
  285.4 4.5 %final_proj.1 = (f32[256,768]{1,0:T(8,128)}, f32[256,768]{1,0:T(8,128)}) custom-call(bf16[128,768]{1,0:T(8,128)(2,1)S(1)} %pad_maximum_fusion.8.refs_0_, bf16[128,768]{1,0:T(8,128)(2,1)S(1)} %collective-permute-done.22.refs_1_, bf16[128,768]{1,0:T(8,128)(2,1)S(1)} %collective-permute-done.23.refs_2_, bf16[128,768]{1,0:T(8,128)(2,1)S(1)} %collective-permute-done.24.refs_3_, ...), custom_call_target="tpu_custom_call" | custom-call | flops 2000000000 | bytes 8000000 | tf_op jit(solution)/shard_map/final_proj/pallas_call | solution.py:730
  294.6 3.0 unpack.1
  (256 shorter events, 64.4 us)
Async XLA Ops:
  7.2 93.9 %all-gather.5.cloned.1.call-start = ((), (), s32[]{:S(2)}) async-start(), calls=%async_computation.2 | async-start | bytes 9289728 | tf_op jit(solution)/shard_map/all_gather | solution.py:846
  11.2 32.9 %collective-permute-start.2 = (bf16[224,768]{1,0:T(8,128)(2,1)S(1)}, bf16[224,768]{1,0:T(8,128)(2,1)S(1)}, u32[]{:S(2)}, u32[]{:S(2)}) collective-permute-start(bf16[224,768]{1,0:T(8,128)(2,1)S(1)} %pad_maximum_fusion.4), channel_id=1, source_target_pairs={{0,1},{1,0},{2,3},{3,2},{4,5},{5,4},{6,7},{7,6},{8,9},{9,8},{10,11... | collective-permute-start | bytes 1032200 | tf_op jit(solution)/shard_map/ppermute | solution.py:838
  11.3 32.8 %collective-permute-start.3 = (bf16[224,768]{1,0:T(8,128)(2,1)S(1)}, bf16[224,768]{1,0:T(8,128)(2,1)S(1)}, u32[]{:S(2)}, u32[]{:S(2)}) collective-permute-start(bf16[224,768]{1,0:T(8,128)(2,1)S(1)} %pad_maximum_fusion.4), channel_id=1, source_target_pairs={{0,2},{1,3},{2,0},{3,1},{4,6},{5,7},{6,4},{7,5},{8,10},{9,11},{10,... | collective-permute-start | bytes 1032200 | tf_op jit(solution)/shard_map/ppermute | solution.py:838
  13.8 30.4 %collective-permute-start.4 = (bf16[224,768]{1,0:T(8,128)(2,1)S(1)}, bf16[224,768]{1,0:T(8,128)(2,1)S(1)}, u32[]{:S(2)}, u32[]{:S(2)}) collective-permute-start(bf16[224,768]{1,0:T(8,128)(2,1)S(1)} %pad_maximum_fusion.4), channel_id=1, source_target_pairs={{0,3},{1,2},{2,1},{3,0},{4,7},{5,6},{6,5},{7,4},{8,11},{9,10},{10,... | collective-permute-start | bytes 1032200 | tf_op jit(solution)/shard_map/ppermute | solution.py:838
  45.2 99.0 %all-gather.7.cloned.1.call-start = ((), (), s32[]{:S(2)}) async-start(), calls=%async_computation.3 | async-start | bytes 3317760 | tf_op jit(solution)/shard_map/all_gather | solution.py:846
  48.7 29.6 %collective-permute-start.9 = (bf16[80,768]{1,0:T(8,128)(2,1)S(1)}, bf16[80,768]{1,0:T(8,128)(2,1)S(1)}, u32[]{:S(2)}, u32[]{:S(2)}) collective-permute-start(bf16[80,768]{1,0:T(8,128)(2,1)S(1)} %constant_dynamic-slice_fusion), channel_id=1, source_target_pairs={{0,2},{1,3},{2,0},{3,1},{4,6},{5,7},{6,4},{7,5},{8,10},{9,11},{10,... | collective-permute-start | bytes 368648 | tf_op jit(solution)/shard_map/ppermute | solution.py:838
  51.1 27.2 %collective-permute-start.10 = (bf16[80,768]{1,0:T(8,128)(2,1)S(1)}, bf16[80,768]{1,0:T(8,128)(2,1)S(1)}, u32[]{:S(2)}, u32[]{:S(2)}) collective-permute-start(bf16[80,768]{1,0:T(8,128)(2,1)S(1)} %constant_dynamic-slice_fusion), channel_id=1, source_target_pairs={{0,3},{1,2},{2,1},{3,0},{4,7},{5,6},{6,5},{7,4},{8,11},{9,10},{10,... | collective-permute-start | bytes 368648 | tf_op jit(solution)/shard_map/ppermute | solution.py:838
  52.0 26.4 %collective-permute-start.5 = (bf16[64,768]{1,0:T(8,128)(2,1)S(1)}, bf16[64,768]{1,0:T(8,128)(2,1)S(1)}, u32[]{:S(2)}, u32[]{:S(2)}) collective-permute-start(bf16[64,768]{1,0:T(8,128)(2,1)S(1)} %copy-done.45), channel_id=1, source_target_pairs={{0,1},{1,0},{2,3},{3,2},{4,5},{5,4},{6,7},{7,6},{8,9},{9,8},{10,11... | collective-permute-start | bytes 294920 | tf_op jit(solution)/shard_map/ppermute | solution.py:838
  53.2 25.1 %collective-permute-start.6 = (bf16[64,768]{1,0:T(8,128)(2,1)S(1)}, bf16[64,768]{1,0:T(8,128)(2,1)S(1)}, u32[]{:S(2)}, u32[]{:S(2)}) collective-permute-start(bf16[64,768]{1,0:T(8,128)(2,1)S(1)} %copy-done.44), channel_id=1, source_target_pairs={{0,2},{1,3},{2,0},{3,1},{4,6},{5,7},{6,4},{7,5},{8,10},{9,11},{10,... | collective-permute-start | bytes 294920 | tf_op jit(solution)/shard_map/ppermute | solution.py:838
  55.4 23.0 %collective-permute-start.7 = (bf16[64,768]{1,0:T(8,128)(2,1)S(1)}, bf16[64,768]{1,0:T(8,128)(2,1)S(1)}, u32[]{:S(2)}, u32[]{:S(2)}) collective-permute-start(bf16[64,768]{1,0:T(8,128)(2,1)S(1)} %copy-done.42), channel_id=1, source_target_pairs={{0,3},{1,2},{2,1},{3,0},{4,7},{5,6},{6,5},{7,4},{8,11},{9,10},{10,... | collective-permute-start | bytes 294920 | tf_op jit(solution)/shard_map/ppermute | solution.py:838
  79.2 145.0 %reduce-scatter.2.cloned.1.call-start = ((), (), s32[]{:S(2)}) async-start(), calls=%async_computation.1 | async-start | bytes 8847360 | tf_op jit(solution)/shard_map/reduce_scatter | solution.py:920
  147.0 29.4 %collective-permute-start.17 = (bf16[4,4,64,768]{3,2,1,0:T(8,128)(2,1)S(1)}, bf16[4,4,64,768]{3,2,1,0:T(8,128)(2,1)S(1)}, u32[]{:S(2)}, u32[]{:S(2)}) collective-permute-start(bf16[4,4,64,768]{3,2,1,0:T(8,128)(2,1)S(1)} %copy-done.33), channel_id=1, source_target_pairs={{0,4},{4,0},{1,5},{5,1},{2,6},{6,2},{3,7},{7,3},{8,12},{12,8},{9,1... | collective-permute-start | bytes 4718600 | tf_op jit(solution)/shard_map/ppermute | solution.py:918
  148.0 28.3 %collective-permute-start.18 = (bf16[64,768]{1,0:T(8,128)(2,1)}, bf16[64,768]{1,0:T(8,128)(2,1)S(1)}, u32[]{:S(2)}, u32[]{:S(2)}) collective-permute-start(bf16[64,768]{1,0:T(8,128)(2,1)} %get-tuple-element.223), channel_id=1, source_target_pairs={{0,1},{1,0},{2,3},{3,2},{4,5},{5,4},{6,7},{7,6},{8,9},{9,8},{10,11... | collective-permute-start | bytes 294920 | tf_op jit(solution)/shard_map/ppermute | solution.py:838
  149.2 27.1 %collective-permute-start.19 = (bf16[64,768]{1,0:T(8,128)(2,1)S(1)}, bf16[64,768]{1,0:T(8,128)(2,1)S(1)}, u32[]{:S(2)}, u32[]{:S(2)}) collective-permute-start(bf16[64,768]{1,0:T(8,128)(2,1)S(1)} %copy-done.40), channel_id=1, source_target_pairs={{0,2},{1,3},{2,0},{3,1},{4,6},{5,7},{6,4},{7,5},{8,10},{9,11},{10,... | collective-permute-start | bytes 294920 | tf_op jit(solution)/shard_map/ppermute | solution.py:838
  151.1 25.3 %collective-permute-start.20 = (bf16[64,768]{1,0:T(8,128)(2,1)S(1)}, bf16[64,768]{1,0:T(8,128)(2,1)S(1)}, u32[]{:S(2)}, u32[]{:S(2)}) collective-permute-start(bf16[64,768]{1,0:T(8,128)(2,1)S(1)} %copy-done.38), channel_id=1, source_target_pairs={{0,3},{1,2},{2,1},{3,0},{4,7},{5,6},{6,5},{7,4},{8,11},{9,10},{10,... | collective-permute-start | bytes 294920 | tf_op jit(solution)/shard_map/ppermute | solution.py:838
  181.2 33.1 %collective-permute-start.23 = (bf16[128,768]{1,0:T(8,128)(2,1)S(1)}, bf16[128,768]{1,0:T(8,128)(2,1)S(1)}, u32[]{:S(2)}, u32[]{:S(2)}) collective-permute-start(bf16[128,768]{1,0:T(8,128)(2,1)S(1)} %pad_maximum_fusion.10), channel_id=1, source_target_pairs={{0,2},{1,3},{2,0},{3,1},{4,6},{5,7},{6,4},{7,5},{8,10},{9,11},{10,... | collective-permute-start | bytes 589832 | tf_op jit(solution)/shard_map/ppermute | solution.py:838
  183.2 31.1 %collective-permute-start.24 = (bf16[128,768]{1,0:T(8,128)(2,1)S(1)}, bf16[128,768]{1,0:T(8,128)(2,1)S(1)}, u32[]{:S(2)}, u32[]{:S(2)}) collective-permute-start(bf16[128,768]{1,0:T(8,128)(2,1)S(1)} %pad_maximum_fusion.11), channel_id=1, source_target_pairs={{0,3},{1,2},{2,1},{3,0},{4,7},{5,6},{6,5},{7,4},{8,11},{9,10},{10,... | collective-permute-start | bytes 589832 | tf_op jit(solution)/shard_map/ppermute | solution.py:838
  183.4 30.9 %collective-permute-start.25 = (bf16[4,64,768]{2,1,0:T(8,128)(2,1)S(1)}, bf16[4,64,768]{2,1,0:T(8,128)(2,1)S(1)}, u32[]{:S(2)}, u32[]{:S(2)}) collective-permute-start(bf16[4,64,768]{2,1,0:T(8,128)(2,1)S(1)} %get-tuple-element.248), channel_id=1, source_target_pairs={{0,8},{8,0},{16,24},{24,16},{1,9},{9,1},{17,25},{25,17},{2,10},{10... | collective-permute-start | bytes 1179656 | tf_op jit(solution)/shard_map/ppermute | solution.py:882
  184.6 29.7 %collective-permute-start.26 = (bf16[4,64,768]{2,1,0:T(8,128)(2,1)S(1)}, bf16[4,64,768]{2,1,0:T(8,128)(2,1)S(1)}, u32[]{:S(2)}, u32[]{:S(2)}) collective-permute-start(bf16[4,64,768]{2,1,0:T(8,128)(2,1)S(1)} %get-tuple-element.249), channel_id=1, source_target_pairs={{0,16},{8,24},{16,0},{24,8},{1,17},{9,25},{17,1},{25,9},{2,18},{10... | collective-permute-start | bytes 1179656 | tf_op jit(solution)/shard_map/ppermute | solution.py:882
  188.7 26.4 %collective-permute-start.27 = (bf16[4,64,768]{2,1,0:T(8,128)(2,1)S(1)}, bf16[4,64,768]{2,1,0:T(8,128)(2,1)}, u32[]{:S(2)}, u32[]{:S(2)}) collective-permute-start(bf16[4,64,768]{2,1,0:T(8,128)(2,1)S(1)} %get-tuple-element.250), channel_id=1, source_target_pairs={{0,24},{8,16},{16,8},{24,0},{1,25},{9,17},{17,9},{25,1},{2,26},{10... | collective-permute-start | bytes 1179656 | tf_op jit(solution)/shard_map/ppermute | solution.py:882
  228.7 28.9 %collective-permute-start.32 = (bf16[224,768]{1,0:T(8,128)(2,1)S(1)}, bf16[224,768]{1,0:T(8,128)(2,1)S(1)}, u32[]{:S(2)}, u32[]{:S(2)}) collective-permute-start(bf16[224,768]{1,0:T(8,128)(2,1)S(1)} %pad_maximum_fusion.5), channel_id=1, source_target_pairs={{0,1},{1,0},{2,3},{3,2},{4,5},{5,4},{6,7},{7,6},{8,9},{9,8},{10,11... | collective-permute-start | bytes 1032200 | tf_op jit(solution)/shard_map/ppermute | solution.py:838
  229.1 28.6 %collective-permute-start.33 = (bf16[224,768]{1,0:T(8,128)(2,1)S(1)}, bf16[224,768]{1,0:T(8,128)(2,1)S(1)}, u32[]{:S(2)}, u32[]{:S(2)}) collective-permute-start(bf16[224,768]{1,0:T(8,128)(2,1)S(1)} %pad_maximum_fusion.6), channel_id=1, source_target_pairs={{0,2},{1,3},{2,0},{3,1},{4,6},{5,7},{6,4},{7,5},{8,10},{9,11},{10,... | collective-permute-start | bytes 1032200 | tf_op jit(solution)/shard_map/ppermute | solution.py:838
  231.3 29.8 %collective-permute-start.34 = (bf16[224,768]{1,0:T(8,128)(2,1)S(1)}, bf16[224,768]{1,0:T(8,128)(2,1)S(1)}, u32[]{:S(2)}, u32[]{:S(2)}) collective-permute-start(bf16[224,768]{1,0:T(8,128)(2,1)S(1)} %pad_maximum_fusion.7), channel_id=1, source_target_pairs={{0,3},{1,2},{2,1},{3,0},{4,7},{5,6},{6,5},{7,4},{8,11},{9,10},{10,... | collective-permute-start | bytes 1032200 | tf_op jit(solution)/shard_map/ppermute | solution.py:838
  261.4 21.7 %collective-permute-start.38 = (bf16[224,768]{1,0:T(8,128)(2,1)S(1)}, bf16[224,768]{1,0:T(8,128)(2,1)S(1)}, u32[]{:S(2)}, u32[]{:S(2)}) collective-permute-start(bf16[224,768]{1,0:T(8,128)(2,1)S(1)} %add_convert_fusion.9), channel_id=1, source_target_pairs={{0,8},{8,0},{16,24},{24,16},{1,9},{9,1},{17,25},{25,17},{2,10},{10... | collective-permute-start | bytes 1032200 | tf_op jit(solution)/shard_map/ppermute | solution.py:882
  (74 other events, 773.3 us)
Sparse Core Ops, SparseCore 0:
  45.3 55.7 all-gather.4
  103.6 31.5 all-gather.6
  145.0 79.0 reduce-scatter.1
where the time goes:
time: 313 us; the launch traced here: 306 us
  Pallas kernels  144 us (46%)
  waiting for transfers between devices  72.9 us (23%)
  starting transfers between devices  43.1 us (14%)
  local copies, waits for them, and re-layouts  15.2 us (5%)
  between operations  15 us (5%)
  other arithmetic  13.5 us (4%)
    pallas_call x2, Pallas kernels, attn_bwd(): pl.pallas_call(attn_bwd_kernel, grid_spec=grid_spec, out_shape=[sds((rr,...  49.4 us
    pallas_call x2, Pallas kernels, attn_fwd(): pl.pallas_call(attn_fwd_kernel, grid_spec=grid_spec, out_shape=[sds((rr,...  45.1 us
    ppermute x27, waiting for transfers between devices, across(): return lax.ppermute(x, 'tensor', [(i, i ^ k) for i in range(n_t)])  31.5 us
    ppermute x27, starting transfers between devices, across(): return lax.ppermute(x, 'tensor', [(i, i ^ k) for i in range(n_t)])  30.1 us
    pallas_call x1, Pallas kernels, ffn(): pl.pallas_call(ffn_kernel, in_specs=[pl.BlockSpec(memory_space=pltpu.SMEM...  28.2 us
    ppermute x8, waiting for transfers between devices, along_dp(): return lax.ppermute(x, 'dp', [(i, i ^ m) for i in range(n_d)])  24.8 us
    pallas_call x1, Pallas kernels, wgrad(): pl.pallas_call(wgrad_kernel, grid=(n_t,), in_specs=[pl.BlockSpec(memory_s...  12.1 us
    reduce_scatter x1, waiting for transfers between devices, body(): ga = lax.psum_scatter(ga, ('dp', 'ctx'), scatter_dimension=0, tiled=True)[0]  9.1 us
  transfers between devices with their start and end apart: 46, of which 13 were waited for; matrix products, arithmetic and copies ran while one was open for 7% of the time, Pallas kernels for 46%

commit v1 on v0

--- a/solution.py
+++ b/solution.py
@@ -599,7 +599,6 @@
     half = n_s * rr
     rows = 2 * half
     sds = jax.ShapeDtypeStruct
-    vm = pl.BlockSpec(memory_space=pltpu.VMEM)
     hbm = pl.BlockSpec(memory_space=pl.ANY)
     big = [
         ((half, D), f32), ((half, D), f32), ((rows, D), f32), ((rows, D), bf16), ((n_t, rows, n_f), bf16),
@@ -607,8 +606,10 @@
     ]
     out = pl.pallas_call(
         ffn_kernel,
-        in_specs=[pl.BlockSpec(memory_space=pltpu.SMEM)] + [vm] * (2 * n_t) + [hbm] * 8 + [vm] * 5,
-        out_specs=[vm] * (2 * n_t) + [hbm] * len(big) + [vm] * 2,
+        grid=(1,),
+        in_specs=[pl.BlockSpec(memory_space=pltpu.SMEM)] + [whole(att0[0].shape)] * (2 * n_t) + [hbm] * 8
+        + [whole((1, D))] * 5,
+        out_specs=[whole(att0[0].shape)] * (2 * n_t) + [hbm] * len(big) + [whole((5, D)), whole((n_t, n_f))],
         out_shape=[sds(att0[0].shape, bf16)] * (2 * n_t) + [sds(*b) for b in big] + [sds((5, D), f32), sds((n_t, n_f), f32)],
         scratch_shapes=[
             pltpu.VMEM((n_t,) + w_inner.shape, bf16), pltpu.VMEM((n_t,) + w_outer.shape, bf16),
@@ -687,14 +688,13 @@
 
 
 def final_kernel(*refs):
-    n_t = (len(refs) - 7) // 2
-    rows = (refs[:n_t], refs[n_t : 2 * n_t])
-    w_own, wgot, dres, gh, gq, w_s, sems = refs[2 * n_t :]
+    n_t = (len(refs) - 10) // 2
+    w_own, wgot, dres, gh, gq, w_s, rows_s, sems, sems_r, sems_d = refs[2 * n_t :]
     n_p = wgot.shape[0]
     half = gh.shape[0]
-    rr = rows[0][0].shape[0] // 2
+    rr = rows_s.shape[1] // 2
     n_h = half // (2 * rr)
-    hc = rows[0][0].shape[1] // (2 * n_h)
+    hc = rows_s.shape[2] // (2 * n_h)
     count = wgot.shape[2]
     copies = [[pltpu.make_async_copy(w_own, w_s.at[0], sems.at[0, 0])]]
     for k in range(1, n_t):
@@ -702,19 +702,23 @@
             pltpu.make_async_copy(wgot.at[j, k - 1], w_s.at[k, pl.ds(j * count, count), :], sems.at[k, j])
             for j in range(n_p)
         ])
-    for per_k in copies:
-        for copy in per_k:
+    row_copies = [pltpu.make_async_copy(refs[i], rows_s.at[i], sems_r.at[i]) for i in range(2 * n_t)]
+    base = [pltpu.make_async_copy(dres.at[pl.ds(i * half, half), :], g, sems_d.at[i]) for i, g in enumerate((gh, gq))]
+    for copy in base:
+        copy.start()
+    for k in range(n_t):
+        for copy in [row_copies[k], row_copies[n_t + k]] + copies[k]:
             copy.start()
-    gh[...] = dres[:half, :]
-    gq[...] = dres[half:, :]
+    for copy in base:
+        copy.wait()
     for k in range(n_t):
-        for copy in copies[k]:
+        for copy in [row_copies[k], row_copies[n_t + k]] + copies[k]:
             copy.wait()
         wq, wk, wv = (w_s[k, i * hc : (i + 1) * hc, :] for i in range(3))
 
         def kind(low, i):
             return jnp.concatenate([
-                rows[side][k][low : low + rr, (2 * s + i) * hc : (2 * s + i + 1) * hc]
+                rows_s[side * n_t + k, low : low + rr, (2 * s + i) * hc : (2 * s + i + 1) * hc]
                 for side in range(2) for s in range(n_h)
             ], 0)
 
@@ -725,73 +729,105 @@
 def final_proj(rows0, rows1, w_own, wgot, dres):
     half = dres.shape[0] // 2
     n_t = len(rows0)
-    vm = pl.BlockSpec(memory_space=pltpu.VMEM)
     hbm = pl.BlockSpec(memory_space=pl.ANY)
     return pl.pallas_call(
         final_kernel,
-        in_specs=[vm] * (2 * n_t) + [hbm, hbm, vm],
+        grid=(1,),
+        in_specs=[hbm] * (2 * n_t + 3),
+        out_specs=[whole((half, D))] * 2,
         out_shape=[jax.ShapeDtypeStruct((half, D), f32)] * 2,
-        scratch_shapes=[pltpu.VMEM((n_t,) + w_own.shape, bf16), pltpu.SemaphoreType.DMA((n_t, wgot.shape[0]))],
-        compiler_params=pltpu.CompilerParams(vmem_limit_bytes=48 << 20),
+        scratch_shapes=[
+            pltpu.VMEM((n_t,) + w_own.shape, bf16), pltpu.VMEM((2 * n_t,) + rows0[0].shape, bf16),
+            pltpu.SemaphoreType.DMA((n_t, wgot.shape[0])), pltpu.SemaphoreType.DMA((2 * n_t,)), pltpu.SemaphoreType.DMA((2,)),
+        ],
+        compiler_params=pltpu.CompilerParams(vmem_limit_bytes=60 << 20),
         cost_estimate=pl.CostEstimate(flops=2 * 10**9, bytes_accessed=8 * 10**6, transcendentals=0),
         name="final_proj",
     )(*rows0, *rows1, w_own, wgot, dres)
 
 
-def unpack_kernel(pos, own, oth, gi, go, gx, gi_s, go_s, gx_s, sems):
+def unpack_kernel(pos, *refs):
+    n_p = len(refs) - 10
+    n_d = n_p // 2
+    gi, go, gw, gx, gi_s, go_s, gx_s, got, sems, sems_g = refs[n_p:]
     d, c = pos[0], pos[1]
-    n_d = own.shape[0]
-    n_p = 2 * n_d
+    hc = gw.shape[0]
     n_i, n_o, n_x = gi_s.shape[0] // n_p, go_s.shape[0] // n_p, gx_s.shape[0] // n_p
+    arrive = []
+    for m in range(n_d):
+        for side in range(2):
+            to = 2 * (m ^ d) + (c if side == 0 else 1 - c)
+            arrive.append(pltpu.make_async_copy(refs[side * n_d + m], got.at[to], sems_g.at[side, m]))
+    for copy in arrive:
+        copy.start()
     copies = []
-    for j in range(n_p):
-        m = d ^ (j // 2)
-        piece = jnp.where(c == j % 2, own[m].astype(f32), oth[m].astype(f32))
-        parts = ((gi_s, gi, n_i, 0), (go_s, go, n_o, n_i), (gx_s, gx, n_x, n_i + n_o))
+    for n, copy in enumerate(arrive):
+        copy.wait()
+        m, side = n // 2, n % 2
+        to = 2 * (m ^ d) + (c if side == 0 else 1 - c)
+        piece = got[to].astype(f32)
+        parts = ((gi_s, gi, n_i, 0), (go_s, go, n_o, n_i), (gx_s, None, n_x, n_i + n_o))
         for i, (src, dst, count, first) in enumerate(parts):
-            rows = slice(j * count, (j + 1) * count)
+            rows = pl.ds(pl.multiple_of(to * count, count), count)
             src[rows, :] = piece[first : first + count]
-            copies.append(pltpu.make_async_copy(src.at[rows, :], dst.at[rows, :], sems.at[i, j]))
-            copies[-1].start()
+            if dst is not None:
+                copies.append(pltpu.make_async_copy(src.at[rows, :], dst.at[rows, :], sems.at[i, n]))
+                copies[-1].start()
+    copies.append(pltpu.make_async_copy(gx_s.at[:hc, :], gw, sems.at[2, 0]))
+    copies[-1].start()
+    gx[...] = gx_s[hc:, :]
     for copy in copies:
         copy.wait()
 
 
-def unpack(pos, own, oth, n_f):
-    vm = pl.BlockSpec(memory_space=pltpu.VMEM)
+def unpack(pos, own, oth, n_f, hc):
     hbm = pl.BlockSpec(memory_space=pl.ANY)
-    shapes = [(D, n_f), (n_f, D), (XROWS, D)]
+    n_p = 2 * len(own)
+    shapes = [(D, n_f), (n_f, D), (hc, D), (XROWS - hc, D)]
     return pl.pallas_call(
         unpack_kernel,
-        in_specs=[pl.BlockSpec(memory_space=pltpu.SMEM), vm, vm],
-        out_specs=[hbm] * 3,
+        grid=(1,),
+        in_specs=[pl.BlockSpec(memory_space=pltpu.SMEM)] + [hbm] * n_p,
+        out_specs=[hbm] * 3 + [pl.BlockSpec(memory_space=pltpu.VMEM)],
         out_shape=[jax.ShapeDtypeStruct(shape, f32) for shape in shapes],
-        scratch_shapes=[pltpu.VMEM(shape, f32) for shape in shapes] + [pltpu.SemaphoreType.DMA((3, 2 * own.shape[0]))],
-        compiler_params=pltpu.CompilerParams(vmem_limit_bytes=48 << 20),
+        scratch_shapes=[
+            pltpu.VMEM((D, n_f), f32), pltpu.VMEM((n_f, D), f32), pltpu.VMEM((XROWS, D), f32),
+            pltpu.VMEM((n_p,) + own[0].shape, bf16), pltpu.SemaphoreType.DMA((3, n_p)),
+            pltpu.SemaphoreType.DMA((2, n_p // 2)),
+        ],
+        compiler_params=pltpu.CompilerParams(vmem_limit_bytes=60 << 20),
         name="unpack",
-    )(pos, own, oth)
-
-
-def unpack_heads_kernel(pos, own, oth, gq, gk, gv, gr, sm):
+    )(pos, *own, *oth)
+
+
+def unpack_heads_kernel(pos, own0, own1, oth0, oth1, gq, gk, gv, gr, b_word, b_rel, b_seg, g_seg):
     c = pos[1]
     hc = gq.shape[0]
     for i, g in enumerate((gq, gk, gv, gr)):
-        rows = slice((i % 2) * hc, (i % 2 + 1) * hc)
-        g[...] = jnp.where(c == i // 2, own[rows, :].astype(f32), oth[rows, :].astype(f32))
-    sums = own[2 * hc :, :hc].astype(f32)
-    sm[...] = sums[:8] + sums[8:]
+        own, oth = ((own0, oth0), (own1, oth1))[i % 2]
+        g[...] = jnp.where(c == i // 2, own[:hc, :].astype(f32), oth[:hc, :].astype(f32))
+    sums = own1[hc:, :hc].astype(f32)
+    sums = sums[:8] + sums[8:]
+    for h in range(hc // DH):
+        cols = slice(h * DH, (h + 1) * DH)
+        for row, dst in enumerate((b_word, b_rel, b_seg)):
+            dst[h : h + 1, :] = sums[row : row + 1, cols]
+        g_seg[h] = sums[3:5, cols]
 
 
 def unpack_heads(pos, own, oth, hc):
-    vm = pl.BlockSpec(memory_space=pltpu.VMEM)
     sds = jax.ShapeDtypeStruct
+    heads = hc // DH
+    shapes = [(hc, D)] * 4 + [(heads, DH)] * 3 + [(heads, 2, DH)]
     return pl.pallas_call(
         unpack_heads_kernel,
-        in_specs=[pl.BlockSpec(memory_space=pltpu.SMEM), vm, vm],
-        out_shape=[sds((hc, D), f32)] * 4 + [sds((8, hc), f32)],
+        grid=(1,),
+        in_specs=[pl.BlockSpec(memory_space=pltpu.SMEM)] + [whole(x.shape) for x in own + oth],
+        out_specs=[whole(shape) for shape in shapes],
+        out_shape=[sds(shape, f32) for shape in shapes],
         compiler_params=pltpu.CompilerParams(vmem_limit_bytes=48 << 20),
         name="unpack_heads",
-    )(pos, own, oth)
+    )(pos, *own, *oth)
 
 
 def table_rows(start, count):
@@ -942,31 +978,33 @@
     total = [jnp.concatenate([ga[k], add(gb[0][k], *[g[k] for g in gb_got])], 0) for k in range(n_t)]
     total_got = [across(total[k], k) for k in range(1, n_t)]
     pay = payload(dq, dkv_own, dkv_oth)
-    part = add(gw0[0], gw1[0], lax.ppermute(add(gw0[1], gw1[1]), "ctx", swap))
-    mask = 1
-    while mask < n_d:
-        part = add(part, along_dp(part, mask))
-        mask *= 2
-    (part,), pay, total_got = tie_all([part], pay, total_got)
+    got_w = lax.ppermute(add(gw0[1], gw1[1]), "ctx", swap)
+    part = [add(gw0[0][:hc], gw1[0][:hc], got_w[:hc]), add(gw0[0][hc:], gw1[0][hc:], got_w[hc:])]
+    masks = [1 << i for i in range(n_d.bit_length() - 1)]
+    for m0, m1 in zip(masks, masks[::-1]):
+        part_got = [along_dp(part[0], m0), along_dp(part[1], m1)]
+        part = [add(part[0], part_got[0]), add(part[1], part_got[1])]
+    part_o = [lax.ppermute(x, "ctx", swap) for x in part]
+    part, part_o, pay, total_got = tie_all(part, part_o, pay, total_got)
     total = add(total[0], *total_got)
 
-    pay, (total, part) = tie_all(pay, [total, part])
+    pay, (total,) = tie_all(pay, [total])
+    others = [along_dp(total, m) for m in range(1, n_d)]
     rows1 = share(pay)
-    others = [along_dp(total, m) for m in range(1, n_d)]
-    *gwt, sm = unpack_heads(pos, part, lax.ppermute(part, "ctx", swap), hc)
-    gwt = [jnp.swapaxes(g, 0, 1) for g in gwt]
-    rows1, others = tie_all(rows1, others)
-    pieces = jnp.stack([total] + others)
+    heads_out = unpack_heads(pos, part, part_o, hc)
+    heads_out, others = tie_all(heads_out, others)
+    gwt = [jnp.swapaxes(g, 0, 1) for g in heads_out[:4]]
+    pieces = [total] + others
+    pieces_o = [lax.ppermute(x, "ctx", swap) for x in pieces]
     grad_h, grad_q = final_proj(rows0, rows1, w_t, wgot_t, dres)
-    g_inner, g_outer, g_x = unpack(pos, pieces, lax.ppermute(pieces, "ctx", swap), n_f)
-    vecs = g_x[hc + 8 : hc + 13, :hc]
-    heads_of = lambda r: r.reshape(heads, DH)
+    g_inner, g_outer, g_wout, g_x = unpack(pos, pieces, pieces_o, n_f, hc)
+    vecs = g_x[8:13, :hc]
     shape = (n_s, rr, D)
     return (
         out_h.reshape(shape), out_q.reshape(shape), grad_h.reshape(shape), grad_q.reshape(shape),
-        gwt[0], gwt[1], gwt[2], gwt[3], g_x[:hc],
-        heads_of(sm[0]), heads_of(sm[1]), heads_of(sm[2]), sm[3:5].reshape(2, heads, DH),
-        vecs[0], vecs[1], g_inner, g_x[hc], g_outer,
+        gwt[0], gwt[1], gwt[2], gwt[3], g_wout,
+        heads_out[4], heads_out[5], heads_out[6], jnp.swapaxes(heads_out[7], 0, 1),
+        vecs[0], vecs[1], g_inner, g_x[0], g_outer,
         vecs[4], vecs[2], vecs[3],
     )
 

time: 313 us -> 311 us (level)
  the two profiles are of different devices: /device:TPU:9 before, /device:TPU:8 now
where the time goes in v1:
time: 311 us; the launch traced here: 305 us
  Pallas kernels  148 us (48%)
  waiting for transfers between devices  63.2 us (20%)
  starting transfers between devices  48.4 us (16%)
  between operations  15.1 us (5%)
  other arithmetic  14.5 us (5%)
  local copies, waits for them, and re-layouts  14.2 us (5%)
    pallas_call x2, Pallas kernels, attn_bwd(): pl.pallas_call(attn_bwd_kernel, grid_spec=grid_spec, out_shape=[sds((rr,...  49.7 us
    pallas_call x2, Pallas kernels, attn_fwd(): pl.pallas_call(attn_fwd_kernel, grid_spec=grid_spec, out_shape=[sds((rr,...  44.9 us
    ppermute x27, starting transfers between devices, across(): return lax.ppermute(x, 'tensor', [(i, i ^ k) for i in range(n_t)])  34.7 us
    ppermute x27, waiting for transfers between devices, across(): return lax.ppermute(x, 'tensor', [(i, i ^ k) for i in range(n_t)])  31.6 us
    pallas_call x1, Pallas kernels, ffn(): pl.pallas_call(ffn_kernel, grid=(1,), in_specs=[pl.BlockSpec(memory_space...  28.2 us
    ppermute x10, waiting for transfers between devices, along_dp(): return lax.ppermute(x, 'dp', [(i, i ^ m) for i in range(n_d)])  17.8 us
    pallas_call x1, Pallas kernels, wgrad(): pl.pallas_call(wgrad_kernel, grid=(n_t,), in_specs=[pl.BlockSpec(memory_s...  12.2 us
    ppermute x10, starting transfers between devices, along_dp(): return lax.ppermute(x, 'dp', [(i, i ^ m) for i in range(n_d)])  11.3 us
  transfers between devices with their start and end apart: 52, of which 18 were waited for; matrix products, arithmetic and copies ran while one was open for 6% of the time, Pallas kernels for 47%

profile of v1, /device:TPU:8, one launch (start us, length us, event | category | flops | bytes accessed | tf_op | source)
XLA Modules:
  0.0 305.3 jit_solution(17571401634888317973)
XLA Ops:
  10.7 3.0 collective-permute-start.3
  20.0 22.5 %attn_fwd.2 = (bf16[64,768]{1,0:T(8,128)(2,1)}, bf16[64,768]{1,0:T(8,128)(2,1)}, bf16[64,768]{1,0:T(8,128)(2,1)}, bf16[64,768]{1,0:T(8,128)(2,1)}, bf16[2,3,2,25...) custom-call(s32[7]{0:T(128)} %get-tuple-element.220.meta, ...), custom_call_target="tpu_custom_call" | custom-call | flops 20000000000 | bytes 32000000 | tf_op jit(solution)/shard_map/attn_fwd/pallas_call | solution.py:216
  48.4 3.0 collective-permute-start.9
  56.2 22.4 %attn_fwd.3 = (bf16[64,768]{1,0:T(8,128)(2,1)}, bf16[64,768]{1,0:T(8,128)(2,1)}, bf16[64,768]{1,0:T(8,128)(2,1)}, bf16[64,768]{1,0:T(8,128)(2,1)}, bf16[2,3,2,25...) custom-call(s32[7]{0:T(128)} %pad_add_fusion.meta, bf16[4,256,768]{2,1,0:T(8,128)(2,1)} %hid.7, ...), custom_call_target="tpu_custom_call" | custom-call | flops 20000000000 | bytes 32000000 | tf_op jit(solution)/shard_map/attn_fwd/pallas_call | solution.py:216
  88.7 4.4 %collective-permute-done.12.refs_6_ = bf16[64,768]{1,0:T(8,128)(2,1)S(1)} collective-permute-done((bf16[64,768]{1,0:T(8,128)(2,1)}, bf16[64,768]{1,0:T(8,128)(2,1)S(1)}, u32[]{:S(2)}, u32[]{:S(2)}) %collective-permute-start.12) | collective-permute-done | bytes 98336 | tf_op jit(solution)/shard_map/ppermute | solution.py:874
  93.0 2.5 collective-permute-done.13.refs_7_
  95.5 5.3 %all-gather.5.cloned.1.call-done = bf16[24,224,768]{2,1,0:T(8,128)(2,1)} async-done(((bf16[3,224,768]{2,1,0:T(8,128)(2,1)}), bf16[24,224,768]{2,1,0:T(8,128)(2,1)}) %all-gather.5.cloned.1.call-update) | async-done | bytes 8257552 | tf_op jit(solution)/shard_map/all_gather | solution.py:882
  100.9 28.2 %ffn.1 = (bf16[64,768]{1,0:T(8,128)(2,1)}, bf16[64,768]{1,0:T(8,128)(2,1)}, bf16[64,768]{1,0:T(8,128)(2,1)}, bf16[64,768]{1,0:T(8,128)(2,1)}, bf16[64,768]{1,0:T...) custom-call(s32[1]{0:T(128)} %bitcast.ti, ...), custom_call_target="tpu_custom_call" | custom-call | flops 20000000000 | bytes 25000000 | tf_op jit(solution)/shard_map/ffn/pallas_call | solution.py:607
  129.6 2.4 collective-permute-start.15
  132.6 12.2 %wgrad.1 = (bf16[8,4,160,768]{3,2,1,0:T(8,128)(2,1)}, bf16[4,4,64,768]{3,2,1,0:T(8,128)(2,1)}, bf16[4,4,64,768]{3,2,1,0:T(8,128)(2,1)}) custom-call(s32[3]{0:T(128)} %pad_add_fusion.3.pos, bf16[512,768]{1,0:T(8,128)(2,1)} %get-tuple-element.206.inner, bf16[4,512,768]{2,1,0:T(8,128)(2,1)} %get-tuple-element.207.act, ...), custom_call_target="tpu_custom_call" | custom-call | flops 6000000000 | bytes 20000000 | tf_op jit(solution)/shard_map/wgrad/pallas_call | solution.py:671
  151.5 25.4 %attn_bwd.2 = (bf16[64,768]{1,0:T(8,128)(2,1)}, bf16[64,768]{1,0:T(8,128)(2,1)}, bf16[64,768]{1,0:T(8,128)(2,1)}, bf16[64,768]{1,0:T(8,128)(2,1)}, bf16[4,64,768...) custom-call(s32[7]{0:T(128)} %get-tuple-element.220.meta, ...), custom_call_target="tpu_custom_call" | custom-call | flops 20000000000 | bytes 32000000 | tf_op jit(solution)/shard_map/attn_bwd/pallas_call | solution.py:406
  186.4 3.8 %collective-permute-done.22.refs_1_ = bf16[128,768]{1,0:T(8,128)(2,1)S(1)} collective-permute-done((bf16[128,768]{1,0:T(8,128)(2,1)S(1)}, bf16[128,768]{1,0:T(8,128)(2,1)S(1)}, u32[]{:S(2)}, u32[]{:S(2)}) %collective-permute-start.22) | collective-permute-done | bytes 196640 | tf_op jit(solution)/shard_map/ppermute | solution.py:874
  191.6 24.3 %attn_bwd.3 = (bf16[64,768]{1,0:T(8,128)(2,1)}, bf16[64,768]{1,0:T(8,128)(2,1)}, bf16[64,768]{1,0:T(8,128)(2,1)}, bf16[64,768]{1,0:T(8,128)(2,1)}, bf16[4,64,768...) custom-call(s32[7]{0:T(128)} %pad_add_fusion.meta, ...), custom_call_target="tpu_custom_call" | custom-call | flops 20000000000 | bytes 32000000 | tf_op jit(solution)/shard_map/attn_bwd/pallas_call | solution.py:406
  216.0 7.5 %reduce-scatter.2.cloned.1.call-done = bf16[1,4,160,768]{3,2,1,0:T(8,128)(2,1)} async-done(((bf16[8,4,160,768]{3,2,1,0:T(8,128)(2,1)}), bf16[1,4,160,768]{3,2,1,0:T(8,128)(2,1)}) %reduce-scatter.2.cloned.1.call-update) | async-done | bytes 983056 | tf_op jit(solution)/shard_map/reduce_scatter | solution.py:956
  226.4 2.5 collective-permute-start.37
  231.2 6.6 %collective-permute-done.29 = bf16[192,768]{1,0:T(8,128)(2,1)S(1)} collective-permute-done((bf16[192,768]{1,0:T(8,128)(2,1)S(1)}, bf16[192,768]{1,0:T(8,128)(2,1)S(1)}, u32[]{:S(2)}, u32[]{:S(2)}) %collective-permute-start.29) | collective-permute-done | bytes 294944 | tf_op jit(solution)/shard_map/ppermute | solution.py:918
  242.0 3.3 %collective-permute-done.30 = bf16[192,768]{1,0:T(8,128)(2,1)S(1)} collective-permute-done((bf16[192,768]{1,0:T(8,128)(2,1)S(1)}, bf16[192,768]{1,0:T(8,128)(2,1)S(1)}, u32[]{:S(2)}, u32[]{:S(2)}) %collective-permute-start.30) | collective-permute-done | bytes 294944 | tf_op jit(solution)/shard_map/ppermute | solution.py:918
  246.8 5.3 %collective-permute-done.37 = bf16[224,768]{1,0:T(8,128)(2,1)S(1)} collective-permute-done((bf16[224,768]{1,0:T(8,128)(2,1)S(1)}, bf16[224,768]{1,0:T(8,128)(2,1)S(1)}, u32[]{:S(2)}, u32[]{:S(2)}) %collective-permute-start.37) | collective-permute-done | bytes 344096 | tf_op jit(solution)/shard_map/ppermute | solution.py:874
  252.1 7.2 %collective-permute-done.38 = bf16[224,768]{1,0:T(8,128)(2,1)S(1)} collective-permute-done((bf16[224,768]{1,0:T(8,128)(2,1)S(1)}, bf16[224,768]{1,0:T(8,128)(2,1)S(1)}, u32[]{:S(2)}, u32[]{:S(2)}) %collective-permute-start.38) | collective-permute-done | bytes 344096 | tf_op jit(solution)/shard_map/ppermute | solution.py:874
  263.1 2.9 collective-permute-start.40
  266.0 4.6 %collective-permute-done.42.refs_1_ = bf16[224,768]{1,0:T(8,128)(2,1)S(1)} collective-permute-done((bf16[224,768]{1,0:T(8,128)(2,1)S(1)}, bf16[224,768]{1,0:T(8,128)(2,1)S(1)}, u32[]{:S(2)}, u32[]{:S(2)}) %collective-permute-start.42) | collective-permute-done | bytes 344096 | tf_op jit(solution)/shard_map/ppermute | solution.py:918
  278.3 3.5 %collective-permute-done.41.refs_7_ = bf16[128,768]{1,0:T(8,128)(2,1)S(1)} collective-permute-done((bf16[128,768]{1,0:T(8,128)(2,1)S(1)}, bf16[128,768]{1,0:T(8,128)(2,1)S(1)}, u32[]{:S(2)}, u32[]{:S(2)}) %collective-permute-start.41) | collective-permute-done | bytes 196640 | tf_op jit(solution)/shard_map/ppermute | solution.py:874
  282.5 6.4 %final_proj.1 = (f32[256,768]{1,0:T(8,128)}, f32[256,768]{1,0:T(8,128)}) custom-call(bf16[128,768]{1,0:T(8,128)(2,1)} %pad_maximum_fusion.7.refs_0_, bf16[128,768]{1,0:T(8,128)(2,1)} %copy-done.41, bf16[128,768]{1,0:T(8,128)(2,1)} %copy-done.42, bf16[128,768]{1,0:T(8,128)(2,1)} %copy-done.43, bf16[128,768]{1,0:T(8,128)(2,1)} %pad_maximum_fusion.11.refs_4_, ...), custom_call_target="tpu_custom_call" | custom-call | flops 2000000000 | bytes 8000000 | tf_op jit(solution)/shard_map/final_proj/pallas_call | solution.py:733
  290.7 5.0 %unpack.1 = (f32[768,768]{1,0:T(8,128)}, f32[768,768]{1,0:T(8,128)}, f32[192,768]{1,0:T(8,128)}, f32[64,768]{1,0:T(8,128)}) custom-call(s32[3]{0:T(128)} %pad_add_fusion.3.pos, bf16[224,768]{1,0:T(8,128)(2,1)} %copy-done.2, bf16[224,768]{1,0:T(8,128)(2,1)} %copy-done.11, bf16[224,768]{1,0:T(8,128)(2,1)} %copy-done.12, bf16[224,768]{1,0:T(8,128)(2,1)} %copy-done.13, ...), custom_call_target="tpu_custom_call" | custom-call | tf_op jit(solution)/shard_map/unpack/pallas_call | solution.py:787
  (284 shorter events, 75.9 us)
Async XLA Ops:
  7.2 93.6 %all-gather.5.cloned.1.call-start = ((), (), s32[]{:S(2)}) async-start(), calls=%async_computation.2 | async-start | bytes 9289728 | tf_op jit(solution)/shard_map/all_gather | solution.py:882
  10.6 31.9 %collective-permute-start.2 = (bf16[224,768]{1,0:T(8,128)(2,1)S(1)}, bf16[224,768]{1,0:T(8,128)(2,1)S(1)}, u32[]{:S(2)}, u32[]{:S(2)}) collective-permute-start(bf16[224,768]{1,0:T(8,128)(2,1)S(1)} %pad_maximum_fusion.3), channel_id=1, source_target_pairs={{0,1},{1,0},{2,3},{3,2},{4,5},{5,4},{6,7},{7,6},{8,9},{9,8},{10,11... | collective-permute-start | bytes 1032200 | tf_op jit(solution)/shard_map/ppermute | solution.py:874
  10.7 31.9 %collective-permute-start.3 = (bf16[224,768]{1,0:T(8,128)(2,1)S(1)}, bf16[224,768]{1,0:T(8,128)(2,1)S(1)}, u32[]{:S(2)}, u32[]{:S(2)}) collective-permute-start(bf16[224,768]{1,0:T(8,128)(2,1)S(1)} %pad_maximum_fusion.3), channel_id=1, source_target_pairs={{0,2},{1,3},{2,0},{3,1},{4,6},{5,7},{6,4},{7,5},{8,10},{9,11},{10,... | collective-permute-start | bytes 1032200 | tf_op jit(solution)/shard_map/ppermute | solution.py:874
  13.7 30.9 %collective-permute-start.4 = (bf16[224,768]{1,0:T(8,128)(2,1)S(1)}, bf16[224,768]{1,0:T(8,128)(2,1)}, u32[]{:S(2)}, u32[]{:S(2)}) collective-permute-start(bf16[224,768]{1,0:T(8,128)(2,1)S(1)} %pad_maximum_fusion.3), channel_id=1, source_target_pairs={{0,3},{1,2},{2,1},{3,0},{4,7},{5,6},{6,5},{7,4},{8,11},{9,10},{10,... | collective-permute-start | bytes 1032200 | tf_op jit(solution)/shard_map/ppermute | solution.py:874
  46.6 98.2 %all-gather.7.cloned.1.call-start = ((), (), s32[]{:S(2)}) async-start(), calls=%async_computation.3 | async-start | bytes 3317760 | tf_op jit(solution)/shard_map/all_gather | solution.py:882
  48.4 30.3 %collective-permute-start.9 = (bf16[80,768]{1,0:T(8,128)(2,1)S(1)}, bf16[80,768]{1,0:T(8,128)(2,1)S(1)}, u32[]{:S(2)}, u32[]{:S(2)}) collective-permute-start(bf16[80,768]{1,0:T(8,128)(2,1)S(1)} %constant_dynamic-slice_fusion), channel_id=1, source_target_pairs={{0,2},{1,3},{2,0},{3,1},{4,6},{5,7},{6,4},{7,5},{8,10},{9,11},{10,... | collective-permute-start | bytes 368648 | tf_op jit(solution)/shard_map/ppermute | solution.py:874
  51.4 27.3 %collective-permute-start.10 = (bf16[80,768]{1,0:T(8,128)(2,1)S(1)}, bf16[80,768]{1,0:T(8,128)(2,1)S(1)}, u32[]{:S(2)}, u32[]{:S(2)}) collective-permute-start(bf16[80,768]{1,0:T(8,128)(2,1)S(1)} %constant_dynamic-slice_fusion), channel_id=1, source_target_pairs={{0,3},{1,2},{2,1},{3,0},{4,7},{5,6},{6,5},{7,4},{8,11},{9,10},{10,... | collective-permute-start | bytes 368648 | tf_op jit(solution)/shard_map/ppermute | solution.py:874
  52.5 26.2 %collective-permute-start.5 = (bf16[64,768]{1,0:T(8,128)(2,1)}, bf16[64,768]{1,0:T(8,128)(2,1)S(1)}, u32[]{:S(2)}, u32[]{:S(2)}) collective-permute-start(bf16[64,768]{1,0:T(8,128)(2,1)} %get-tuple-element.183), channel_id=1, source_target_pairs={{0,1},{1,0},{2,3},{3,2},{4,5},{5,4},{6,7},{7,6},{8,9},{9,8},{10,11... | collective-permute-start | bytes 294920 | tf_op jit(solution)/shard_map/ppermute | solution.py:874
  53.5 25.2 %collective-permute-start.6 = (bf16[64,768]{1,0:T(8,128)(2,1)}, bf16[64,768]{1,0:T(8,128)(2,1)S(1)}, u32[]{:S(2)}, u32[]{:S(2)}) collective-permute-start(bf16[64,768]{1,0:T(8,128)(2,1)} %get-tuple-element.184), channel_id=1, source_target_pairs={{0,2},{1,3},{2,0},{3,1},{4,6},{5,7},{6,4},{7,5},{8,10},{9,11},{10,... | collective-permute-start | bytes 294920 | tf_op jit(solution)/shard_map/ppermute | solution.py:874
  55.6 23.2 %collective-permute-start.7 = (bf16[64,768]{1,0:T(8,128)(2,1)S(1)}, bf16[64,768]{1,0:T(8,128)(2,1)S(1)}, u32[]{:S(2)}, u32[]{:S(2)}) collective-permute-start(bf16[64,768]{1,0:T(8,128)(2,1)S(1)} %copy-done.55), channel_id=1, source_target_pairs={{0,3},{1,2},{2,1},{3,0},{4,7},{5,6},{6,5},{7,4},{8,11},{9,10},{10,... | collective-permute-start | bytes 294920 | tf_op jit(solution)/shard_map/ppermute | solution.py:874
  79.5 144.0 %reduce-scatter.2.cloned.1.call-start = ((), (), s32[]{:S(2)}) async-start(), calls=%async_computation.1 | async-start | bytes 8847360 | tf_op jit(solution)/shard_map/reduce_scatter | solution.py:956
  147.6 29.4 %collective-permute-start.17 = (bf16[4,4,64,768]{3,2,1,0:T(8,128)(2,1)S(1)}, bf16[4,4,64,768]{3,2,1,0:T(8,128)(2,1)S(1)}, u32[]{:S(2)}, u32[]{:S(2)}) collective-permute-start(bf16[4,4,64,768]{3,2,1,0:T(8,128)(2,1)S(1)} %copy-done.38), channel_id=1, source_target_pairs={{0,4},{4,0},{1,5},{5,1},{2,6},{6,2},{3,7},{7,3},{8,12},{12,8},{9,1... | collective-permute-start | bytes 4718600 | tf_op jit(solution)/shard_map/ppermute | solution.py:954
  147.6 29.3 %collective-permute-start.18 = (bf16[64,768]{1,0:T(8,128)(2,1)S(1)}, bf16[64,768]{1,0:T(8,128)(2,1)S(1)}, u32[]{:S(2)}, u32[]{:S(2)}) collective-permute-start(bf16[64,768]{1,0:T(8,128)(2,1)S(1)} %copy-done.54), channel_id=1, source_target_pairs={{0,1},{1,0},{2,3},{3,2},{4,5},{5,4},{6,7},{7,6},{8,9},{9,8},{10,11... | collective-permute-start | bytes 294920 | tf_op jit(solution)/shard_map/ppermute | solution.py:874
  149.0 27.9 %collective-permute-start.19 = (bf16[64,768]{1,0:T(8,128)(2,1)S(1)}, bf16[64,768]{1,0:T(8,128)(2,1)S(1)}, u32[]{:S(2)}, u32[]{:S(2)}) collective-permute-start(bf16[64,768]{1,0:T(8,128)(2,1)S(1)} %copy-done.52), channel_id=1, source_target_pairs={{0,2},{1,3},{2,0},{3,1},{4,6},{5,7},{6,4},{7,5},{8,10},{9,11},{10,... | collective-permute-start | bytes 294920 | tf_op jit(solution)/shard_map/ppermute | solution.py:874
  150.9 26.0 %collective-permute-start.20 = (bf16[64,768]{1,0:T(8,128)(2,1)S(1)}, bf16[64,768]{1,0:T(8,128)(2,1)S(1)}, u32[]{:S(2)}, u32[]{:S(2)}) collective-permute-start(bf16[64,768]{1,0:T(8,128)(2,1)S(1)} %copy-done.50), channel_id=1, source_target_pairs={{0,3},{1,2},{2,1},{3,0},{4,7},{5,6},{6,5},{7,4},{8,11},{9,10},{10,... | collective-permute-start | bytes 294920 | tf_op jit(solution)/shard_map/ppermute | solution.py:874
  182.1 33.9 %collective-permute-start.23 = (bf16[128,768]{1,0:T(8,128)(2,1)S(1)}, bf16[128,768]{1,0:T(8,128)(2,1)S(1)}, u32[]{:S(2)}, u32[]{:S(2)}) collective-permute-start(bf16[128,768]{1,0:T(8,128)(2,1)S(1)} %pad_maximum_fusion.9), channel_id=1, source_target_pairs={{0,2},{1,3},{2,0},{3,1},{4,6},{5,7},{6,4},{7,5},{8,10},{9,11},{10,... | collective-permute-start | bytes 589832 | tf_op jit(solution)/shard_map/ppermute | solution.py:874
  183.9 32.1 %collective-permute-start.24 = (bf16[128,768]{1,0:T(8,128)(2,1)S(1)}, bf16[128,768]{1,0:T(8,128)(2,1)S(1)}, u32[]{:S(2)}, u32[]{:S(2)}) collective-permute-start(bf16[128,768]{1,0:T(8,128)(2,1)S(1)} %pad_maximum_fusion.10), channel_id=1, source_target_pairs={{0,3},{1,2},{2,1},{3,0},{4,7},{5,6},{6,5},{7,4},{8,11},{9,10},{10,... | collective-permute-start | bytes 589832 | tf_op jit(solution)/shard_map/ppermute | solution.py:874
  184.4 31.6 %collective-permute-start.25 = (bf16[4,64,768]{2,1,0:T(8,128)(2,1)S(1)}, bf16[4,64,768]{2,1,0:T(8,128)(2,1)S(1)}, u32[]{:S(2)}, u32[]{:S(2)}) collective-permute-start(bf16[4,64,768]{2,1,0:T(8,128)(2,1)S(1)} %get-tuple-element.258), channel_id=1, source_target_pairs={{0,8},{8,0},{16,24},{24,16},{1,9},{9,1},{17,25},{25,17},{2,10},{10... | collective-permute-start | bytes 1179656 | tf_op jit(solution)/shard_map/ppermute | solution.py:918
  185.9 30.1 %collective-permute-start.26 = (bf16[4,64,768]{2,1,0:T(8,128)(2,1)S(1)}, bf16[4,64,768]{2,1,0:T(8,128)(2,1)S(1)}, u32[]{:S(2)}, u32[]{:S(2)}) collective-permute-start(bf16[4,64,768]{2,1,0:T(8,128)(2,1)S(1)} %get-tuple-element.259), channel_id=1, source_target_pairs={{0,16},{8,24},{16,0},{24,8},{1,17},{9,25},{17,1},{25,9},{2,18},{10... | collective-permute-start | bytes 1179656 | tf_op jit(solution)/shard_map/ppermute | solution.py:918
  190.2 25.8 %collective-permute-start.27 = (bf16[4,64,768]{2,1,0:T(8,128)(2,1)S(1)}, bf16[4,64,768]{2,1,0:T(8,128)(2,1)S(1)}, u32[]{:S(2)}, u32[]{:S(2)}) collective-permute-start(bf16[4,64,768]{2,1,0:T(8,128)(2,1)S(1)} %get-tuple-element.260), channel_id=1, source_target_pairs={{0,24},{8,16},{16,8},{24,0},{1,25},{9,17},{17,9},{25,1},{2,26},{10... | collective-permute-start | bytes 1179656 | tf_op jit(solution)/shard_map/ppermute | solution.py:918
  225.8 21.0 %collective-permute-start.36 = (bf16[224,768]{1,0:T(8,128)(2,1)S(1)}, bf16[224,768]{1,0:T(8,128)(2,1)S(1)}, u32[]{:S(2)}, u32[]{:S(2)}) collective-permute-start(bf16[224,768]{1,0:T(8,128)(2,1)S(1)} %pad_maximum_fusion.4), channel_id=1, source_target_pairs={{0,1},{1,0},{2,3},{3,2},{4,5},{5,4},{6,7},{7,6},{8,9},{9,8},{10,11... | collective-permute-start | bytes 1032200 | tf_op jit(solution)/shard_map/ppermute | solution.py:874
  226.4 25.7 %collective-permute-start.37 = (bf16[224,768]{1,0:T(8,128)(2,1)S(1)}, bf16[224,768]{1,0:T(8,128)(2,1)S(1)}, u32[]{:S(2)}, u32[]{:S(2)}) collective-permute-start(bf16[224,768]{1,0:T(8,128)(2,1)S(1)} %pad_maximum_fusion.5), channel_id=1, source_target_pairs={{0,2},{1,3},{2,0},{3,1},{4,6},{5,7},{6,4},{7,5},{8,10},{9,11},{10,... | collective-permute-start | bytes 1032200 | tf_op jit(solution)/shard_map/ppermute | solution.py:874
  228.9 30.4 %collective-permute-start.38 = (bf16[224,768]{1,0:T(8,128)(2,1)S(1)}, bf16[224,768]{1,0:T(8,128)(2,1)S(1)}, u32[]{:S(2)}, u32[]{:S(2)}) collective-permute-start(bf16[224,768]{1,0:T(8,128)(2,1)S(1)} %pad_maximum_fusion.6), channel_id=1, source_target_pairs={{0,3},{1,2},{2,1},{3,0},{4,7},{5,6},{6,5},{7,4},{8,11},{9,10},{10,... | collective-permute-start | bytes 1032200 | tf_op jit(solution)/shard_map/ppermute | solution.py:874
  260.1 16.0 %collective-permute-start.43 = (bf16[224,768]{1,0:T(8,128)(2,1)S(1)}, bf16[224,768]{1,0:T(8,128)(2,1)S(1)}, u32[]{:S(2)}, u32[]{:S(2)}) collective-permute-start(bf16[224,768]{1,0:T(8,128)(2,1)S(1)} %add_convert_fusion.6.refs_0_), channel_id=1, source_target_pairs={{0,16},{8,24},{16,0},{24,8},{1,17},{9,25},{17,1},{25,9},{2,18},{10... | collective-permute-start | bytes 1032200 | tf_op jit(solution)/shard_map/ppermute | solution.py:918
  (91 other events, 934.3 us)
Sparse Core Ops, SparseCore 0:
  46.8 54.0 all-gather.4
  103.3 31.4 all-gather.6
  145.0 78.4 reduce-scatter.1
